TPU v7x, 128 devices: a whole 4x4x4 slice. The times are simulated.
128 devices in a mesh: sx: 8 (over y_hi, x), sy: 8 (over z, core), par: 2 (over y_lo).
Axes of the slice: x: 4, y: 4 (y_hi: 2, y_lo: 2; y = y_hi * 2 + y_lo), z: 4, core: 2. Of those that a mesh axis runs over, the one named last changes fastest.
Arguments:
- initial_state: float32 [64, 128, 128, 128], P('par', 'sx', 'sy'), may hold values from -6 to 6
- conductivity: float32 [64, 128, 128, 128], P('par', 'sx', 'sy'), may hold values from 0.1 to 1
- omega: bfloat16 [64, 64], replicated, may hold values from -0.75 to 0.75
- psi: bfloat16 [64, 128, 128, 128], P(None, 'sx', 'sy'), may hold values from -0.01171875 to 0.01171875
- range_prev: bfloat16 [64, 128, 128, 128], P('par', 'sx', 'sy'), may hold values from -3 to 3
- corange_prev: float32 [64, 64], P(None, 'par'), may hold values from -3 to 3
Outputs:
- final_state: float32 [64, 128, 128, 128], P('par', 'sx', 'sy')
- range_sketch: bfloat16 [64, 128, 128, 128], P('par', 'sx', 'sy')
- corange_sketch: float32 [64, 64], P(None, 'par')
All inputs are finite; a program needn't handle non-finite values.
Results may differ from a plain program's by a relative error of at most 0.0033.
Values may be sent and summed in bfloat16 or wider, within the bound.
A program may use at most 192 MiB of HBM per device.

v0:
```python
import jax
import jax.numpy as jnp
from jax import lax
from jax.sharding import PartitionSpec as P

STEPS = 4


def extended(block, sides, width):
    for axis, dim in sides:
        count = lax.axis_size(axis)
        forward = [(i, i + 1) for i in range(count - 1)]
        backward = [(target, source) for source, target in forward]
        low = lax.ppermute(
            lax.slice_in_dim(block, block.shape[dim] - width, None, axis=dim), axis, forward
        )
        high = lax.ppermute(lax.slice_in_dim(block, 0, width, axis=dim), axis, backward)
        block = jnp.concatenate([low, block, high], axis=dim)
    return block


def advance(field, kpad):
    center = field[:, 1:-1, 1:-1, :]
    kcen = kpad[:, 1:-1, 1:-1, :]
    width_x = center.shape[1]
    width_y = center.shape[2]
    zfield = jnp.pad(center, ((0, 0), (0, 0), (0, 0), (1, 1)))
    zcond = jnp.pad(kcen, ((0, 0), (0, 0), (0, 0), (1, 1)))
    length = center.shape[3]
    pairs = [
        (field[:, 2:, 1:-1, :], kpad[:, 2:, 1:-1, :]),
        (field[:, :width_x, 1:-1, :], kpad[:, :width_x, 1:-1, :]),
        (field[:, 1:-1, 2:, :], kpad[:, 1:-1, 2:, :]),
        (field[:, 1:-1, :width_y, :], kpad[:, 1:-1, :width_y, :]),
        (zfield[:, :, :, 2:], zcond[:, :, :, 2:]),
        (zfield[:, :, :, :length], zcond[:, :, :, :length]),
    ]
    total = jnp.zeros_like(center)
    for unb, knb in pairs:
        total = total + 0.5 * (kcen + knb) * (unb - center)
    return center + 0.16 * total


def per_device(initial_state, conductivity, omega, psi, range_prev, corange_prev):
    samples, cells_x, cells_y, length = initial_state.shape
    kpad = extended(conductivity, (("sx", 1), ("sy", 2)), 1)
    state = initial_state
    for step in range(STEPS):
        field = extended(state, (("sx", 1), ("sy", 2)), 1)
        state = advance(field, kpad)
    snapshot = state.astype(jnp.bfloat16)
    flat_snap = snapshot.reshape(samples, cells_x * cells_y * length)
    rank = omega.shape[1]
    rank_dev = range_prev.shape[0]
    own_cols = lax.dynamic_slice_in_dim(omega, lax.axis_index("par") * rank_dev, rank_dev, 1)
    start_sum = range_prev.astype(jnp.float32)
    piece = lax.all_gather(snapshot, "par", axis=0, tiled=True)
    rows = piece.shape[0]
    term = lax.dot_general(
        own_cols,
        piece.reshape(rows, -1),
        (((0,), (0,)), ((), ())),
        preferred_element_type=jnp.float32,
    )
    range_sum = start_sum + term.reshape(start_sum.shape)
    range_sketch = range_sum.astype(jnp.bfloat16)
    flat_psi = psi.reshape(rank, cells_x * cells_y * length)
    partial_value = lax.dot_general(
        flat_psi, flat_snap, (((1,), (1,)), ((), ())), preferred_element_type=jnp.float32
    )
    corange_sketch = corange_prev + lax.psum(partial_value, ("sx", "sy"))
    return (state, range_sketch, corange_sketch)


def solution(mesh):
    in_specs = (
        P("par", "sx", "sy", None),
        P("par", "sx", "sy", None),
        P(),
        P(None, "sx", "sy", None),
        P("par", "sx", "sy", None),
        P(None, "par"),
    )
    out_specs = (P("par", "sx", "sy", None), P("par", "sx", "sy", None), P(None, "par"))
    return jax.shard_map(
        per_device, mesh=mesh, in_specs=in_specs, out_specs=out_specs, check_vma=False
    )
```

profile of v0, /device:TPU:24, one launch (start us, length us, event | category | flops | bytes accessed | tf_op | source)
XLA Modules:
  0.0 525.8 jit_solution(14510973290693297946)
XLA Ops:
  7.2 4.8 copy.22
  12.0 3.4 collective-permute-start.2
  15.5 6.3 %collective-permute-start = (f32[32,1,16,128]{3,0,2,1:T(8,128)S(1)}, f32[32,1,16,128]{3,0,2,1:T(8,128)S(1)}, u32[]{:S(2)}, u32[]{:S(2)}) collective-permute-start(f32[32,1,16,128]{3,0,2,1:T(8,128)S(1)} %get-tuple-element.31), channel_id=1, source_target_pairs={{16,0},{32,16},{48,32},{64,48},{80,64},{96,80},{112,96},{17,1},{33... | collective-permute-start | bytes 786440 | tf_op jit(solution)/shard_map/ppermute | solution.py:17
  21.8 2.4 copy.44
  26.2 7.5 %collective-permute-start.1 = (f32[32,1,16,128]{3,0,2,1:T(8,128)S(1)}, f32[32,1,16,128]{3,0,2,1:T(8,128)S(1)}, u32[]{:S(2)}, u32[]{:S(2)}) collective-permute-start(f32[32,1,16,128]{3,0,2,1:T(8,128)S(1)} %get-tuple-element.32), channel_id=1, source_target_pairs={{16,0},{32,16},{48,32},{64,48},{80,64},{96,80},{112,96},{17,1},{33... | collective-permute-start | bytes 786440 | tf_op jit(solution)/shard_map/ppermute | solution.py:17
  33.8 2.4 constant_dynamic-update-slice_fusion.1
  37.6 3.0 collective-permute-start.6
  41.4 4.4 constant_dynamic-update-slice_fusion.4
  48.9 4.3 collective-permute-start.7
  54.2 10.3 %fusion.9 = f32[32,16,16,128]{3,0,2,1:T(8,128)S(1)} fusion(f32[32,16,16,128]{3,0,2,1:T(8,128)S(1)} %copy.44, f32[32,18,16,128]{3,0,2,1:T(8,128)} %constant_dynamic-update-slice_fusion.3, f32[32,18,1,128]{3,0,2,1:T(8,128)S(1)} %collective-permute-done.7, f32[32,18,1,128]{3,0,2,1:T(8,128)S(1)} %collective-permute-done.5, ...), kind=kLoop, calls=%fused_computation.19 | loop fusion | flops 40894464 | bytes 24248320 | tf_op jit(solution)/shard_map/add | solution.py:41
  66.5 3.9 collective-permute-start.9
  70.4 2.4 collective-permute-done.8
  72.8 5.5 %collective-permute-done.9 = f32[32,1,16,128]{3,0,2,1:T(8,128)S(1)} collective-permute-done((f32[32,1,16,128]{3,0,2,1:T(8,128)S(1)}, f32[32,1,16,128]{3,0,2,1:T(8,128)S(1)}, u32[]{:S(2)}, u32[]{:S(2)}) %collective-permute-start.9) | collective-permute-done | bytes 262176 | tf_op jit(solution)/shard_map/ppermute | solution.py:14
  79.7 5.6 %collective-permute-start.11 = (f32[32,18,1,128]{3,0,2,1:T(8,128)S(1)}, f32[32,18,1,128]{3,0,2,1:T(8,128)S(1)}, u32[]{:S(2)}, u32[]{:S(2)}) collective-permute-start(f32[32,18,1,128]{3,0,2,1:T(8,128)S(1)} %get-tuple-element.19), channel_id=1, source_target_pairs={{0,2},{2,4},{4,6},{6,8},{8,10},{10,12},{12,14},{1,3},{3,5},{5,7},{... | collective-permute-start | bytes 884744 | tf_op jit(solution)/shard_map/ppermute | solution.py:14
  86.5 8.1 %fusion.17 = f32[32,16,16,128]{3,0,2,1:T(8,128)S(1)} fusion(f32[32,16,16,128]{3,0,2,1:T(8,128)S(1)} %fusion.9, f32[32,18,1,128]{3,0,2,1:T(8,128)S(1)} %collective-permute-done.11, f32[32,1,16,128]{3,0,2,1:T(8,128)S(1)} %collective-permute-done.8, f32[32,1,16,128]{3,0,2,1:T(8,128)S(1)} %collective-permute-done.9, ...), kind=kLoop, calls=%fused_computation.27 | loop fusion | flops 45088768 | bytes 19529728 | tf_op jit(solution)/shard_map/add | solution.py:41
  96.5 3.9 collective-permute-start.13
  100.5 2.4 collective-permute-done.12
  102.9 5.5 %collective-permute-done.13 = f32[32,1,16,128]{3,0,2,1:T(8,128)S(1)} collective-permute-done((f32[32,1,16,128]{3,0,2,1:T(8,128)S(1)}, f32[32,1,16,128]{3,0,2,1:T(8,128)S(1)}, u32[]{:S(2)}, u32[]{:S(2)}) %collective-permute-start.13) | collective-permute-done | bytes 262176 | tf_op jit(solution)/shard_map/ppermute | solution.py:14
  109.8 8.9 %collective-permute-start.15 = (f32[32,18,1,128]{3,0,2,1:T(8,128)S(1)}, f32[32,18,1,128]{3,0,2,1:T(8,128)S(1)}, u32[]{:S(2)}, u32[]{:S(2)}) collective-permute-start(f32[32,18,1,128]{3,0,2,1:T(8,128)S(1)} %get-tuple-element.17), channel_id=1, source_target_pairs={{0,2},{2,4},{4,6},{6,8},{8,10},{10,12},{12,14},{1,3},{3,5},{5,7},{... | collective-permute-start | bytes 884744 | tf_op jit(solution)/shard_map/ppermute | solution.py:14
  119.8 8.1 %fusion.25 = f32[32,16,16,128]{3,0,2,1:T(8,128)S(1)} fusion(f32[32,16,16,128]{3,0,2,1:T(8,128)S(1)} %fusion.17, f32[32,18,1,128]{3,0,2,1:T(8,128)S(1)} %collective-permute-done.15, f32[32,1,16,128]{3,0,2,1:T(8,128)S(1)} %collective-permute-done.12, f32[32,1,16,128]{3,0,2,1:T(8,128)S(1)} %collective-permute-done.13, ...), kind=kLoop, calls=%fused_computation.35 | loop fusion | flops 45088768 | bytes 19529728 | tf_op jit(solution)/shard_map/add | solution.py:41
  129.9 3.9 collective-permute-start.17
  133.8 2.4 collective-permute-done.16
  136.2 5.5 %collective-permute-done.17 = f32[32,1,16,128]{3,0,2,1:T(8,128)S(1)} collective-permute-done((f32[32,1,16,128]{3,0,2,1:T(8,128)S(1)}, f32[32,1,16,128]{3,0,2,1:T(8,128)S(1)}, u32[]{:S(2)}, u32[]{:S(2)}) %collective-permute-start.17) | collective-permute-done | bytes 262176 | tf_op jit(solution)/shard_map/ppermute | solution.py:14
  143.1 8.6 %collective-permute-start.19 = (f32[32,18,1,128]{3,0,2,1:T(8,128)S(1)}, f32[32,18,1,128]{3,0,2,1:T(8,128)S(1)}, u32[]{:S(2)}, u32[]{:S(2)}) collective-permute-start(f32[32,18,1,128]{3,0,2,1:T(8,128)S(1)} %get-tuple-element.15), channel_id=1, source_target_pairs={{0,2},{2,4},{4,6},{6,8},{8,10},{10,12},{12,14},{1,3},{3,5},{5,7},{... | collective-permute-start | bytes 884744 | tf_op jit(solution)/shard_map/ppermute | solution.py:14
  152.9 9.7 %fusion.100 = (bf16[32,16,16,128]{3,0,2,1:T(8,128)(2,1)S(1)}, f32[32,16,16,128]{3,0,2,1:T(8,128)}) fusion(f32[32,16,16,128]{3,0,2,1:T(8,128)S(1)} %fusion.25, f32[32,16,16,128]{3,0,2,1:T(8,128)S(1)} %copy.22, f32[32,1,16,128]{3,0,2,1:T(8,128)S(1)} %collective-permute-done.16, f32[32,1,16,128]{3,0,2,1:T(8,128)S(1)} %collective-permute-done.17, ...), kind=kLoop, calls=%fused_computation.155 | loop fusion | flops 46137344 | bytes 21626880 | tf_op jit(solution)/shard_map/convert_element_type | solution.py:51
  162.6 2.1 copy.47
  164.8 6.8 %copy.50 = f32[32,16,16,128]{3,2,1,0:T(8,128)} copy(f32[32,16,16,128]{3,0,2,1:T(8,128)} %get-tuple-element.13) | data formatting | bytes 8388608
  171.6 3.7 fusion.94
  175.3 330.3 %psum.7 = f32[64,32]{0,1:T(8,128)S(1)} all-reduce(f32[64,32]{0,1:T(8,128)S(1)} %fusion.94), channel_id=1, replica_groups=mesh['sx'=8,'sy'=8,'par'=2] {'sx','sy'}, use_global_device_ids=true, to_apply=%region_0.1 | all-reduce | flops 2048 | bytes 16384 | tf_op jit(solution)/shard_map/psum | solution.py:71
  506.2 4.9 copy.69
  512.7 4.1 add_convert_fusion
  516.8 2.1 copy.51
  (54 shorter events, 23.8 us)
Async XLA Ops:
  7.2 505.2 %copy-start = (bf16[64,64]{1,0:T(8,128)(2,1)S(1)}, bf16[64,64]{1,0:T(8,128)(2,1)}, u32[]{:S(2)}) copy-start(bf16[64,64]{1,0:T(8,128)(2,1)} %param.8) | copy-start | bytes 24580
  7.2 499.1 %all-gather.2.cloned.1.call-start = ((), (), s32[]{:S(2)}) async-start(), calls=%async_computation | async-start | bytes 6291456 | tf_op jit(solution)/shard_map/all_gather | solution.py:57
  7.2 14.6 %copy-start.2 = (f32[32,16,16,128]{3,2,1,0:T(8,128)S(1)}, f32[32,16,16,128]{3,2,1,0:T(8,128)}, u32[]{:S(2)}) copy-start(f32[32,16,16,128]{3,2,1,0:T(8,128)} %param.6) | copy-start | bytes 12582916
  12.0 21.7 %collective-permute-start.2 = (f32[32,1,16,128]{3,0,2,1:T(8,128)S(1)}, f32[32,1,16,128]{3,0,2,1:T(8,128)S(1)}, u32[]{:S(2)}, u32[]{:S(2)}) collective-permute-start(f32[32,1,16,128]{3,0,2,1:T(8,128)S(1)} %get-tuple-element.30), channel_id=1, source_target_pairs={{0,16},{16,32},{32,48},{48,64},{64,80},{80,96},{96,112},{1,17},{17... | collective-permute-start | bytes 786440 | tf_op jit(solution)/shard_map/ppermute | solution.py:14
  15.5 18.3 %copy-start.1 = (f32[32,16,16,128]{3,2,1,0:T(8,128)S(1)}, f32[32,16,16,128]{3,2,1,0:T(8,128)}, u32[]{:S(2)}) copy-start(f32[32,16,16,128]{3,2,1,0:T(8,128)} %param.7) | copy-start | bytes 12582916
  15.5 20.8 %collective-permute-start = (f32[32,1,16,128]{3,0,2,1:T(8,128)S(1)}, f32[32,1,16,128]{3,0,2,1:T(8,128)S(1)}, u32[]{:S(2)}, u32[]{:S(2)}) collective-permute-start(f32[32,1,16,128]{3,0,2,1:T(8,128)S(1)} %get-tuple-element.31), channel_id=1, source_target_pairs={{16,0},{32,16},{48,32},{64,48},{80,64},{96,80},{112,96},{17,1},{33... | collective-permute-start | bytes 786440 | tf_op jit(solution)/shard_map/ppermute | solution.py:17
  24.3 16.4 %collective-permute-start.3 = (f32[32,1,16,128]{3,0,2,1:T(8,128)S(1)}, f32[32,1,16,128]{3,0,2,1:T(8,128)S(1)}, u32[]{:S(2)}, u32[]{:S(2)}) collective-permute-start(f32[32,1,16,128]{3,0,2,1:T(8,128)S(1)} %get-tuple-element.33), channel_id=1, source_target_pairs={{0,16},{16,32},{32,48},{48,64},{64,80},{80,96},{96,112},{1,17},{17... | collective-permute-start | bytes 786440 | tf_op jit(solution)/shard_map/ppermute | solution.py:14
  26.2 19.6 %collective-permute-start.1 = (f32[32,1,16,128]{3,0,2,1:T(8,128)S(1)}, f32[32,1,16,128]{3,0,2,1:T(8,128)S(1)}, u32[]{:S(2)}, u32[]{:S(2)}) collective-permute-start(f32[32,1,16,128]{3,0,2,1:T(8,128)S(1)} %get-tuple-element.32), channel_id=1, source_target_pairs={{16,0},{32,16},{48,32},{64,48},{80,64},{96,80},{112,96},{17,1},{33... | collective-permute-start | bytes 786440 | tf_op jit(solution)/shard_map/ppermute | solution.py:17
  36.3 16.9 %collective-permute-start.4 = (f32[32,18,1,128]{3,0,2,1:T(8,128)S(1)}, f32[32,18,1,128]{3,0,2,1:T(8,128)S(1)}, u32[]{:S(2)}, u32[]{:S(2)}) collective-permute-start(f32[32,18,1,128]{3,0,2,1:T(8,128)S(1)} %get-tuple-element.21), channel_id=1, source_target_pairs={{2,0},{4,2},{6,4},{8,6},{10,8},{12,10},{14,12},{3,1},{5,3},{7,5},{... | collective-permute-start | bytes 884744 | tf_op jit(solution)/shard_map/ppermute | solution.py:17
  37.6 15.6 %collective-permute-start.6 = (f32[32,18,1,128]{3,0,2,1:T(8,128)S(1)}, f32[32,18,1,128]{3,0,2,1:T(8,128)S(1)}, u32[]{:S(2)}, u32[]{:S(2)}) collective-permute-start(f32[32,18,1,128]{3,0,2,1:T(8,128)S(1)} %get-tuple-element.20), channel_id=1, source_target_pairs={{0,2},{2,4},{4,6},{6,8},{8,10},{10,12},{12,14},{1,3},{3,5},{5,7},{... | collective-permute-start | bytes 884744 | tf_op jit(solution)/shard_map/ppermute | solution.py:14
  47.6 5.6 %collective-permute-start.5 = (f32[32,18,1,128]{3,0,2,1:T(8,128)S(1)}, f32[32,18,1,128]{3,0,2,1:T(8,128)S(1)}, u32[]{:S(2)}, u32[]{:S(2)}) collective-permute-start(f32[32,18,1,128]{3,0,2,1:T(8,128)S(1)} %get-tuple-element.22), channel_id=1, source_target_pairs={{2,0},{4,2},{6,4},{8,6},{10,8},{12,10},{14,12},{3,1},{5,3},{7,5},{... | collective-permute-start | bytes 884744 | tf_op jit(solution)/shard_map/ppermute | solution.py:17
  48.9 5.3 collective-permute-start.7
  64.5 8.3 %collective-permute-start.8 = (f32[32,1,16,128]{3,0,2,1:T(8,128)S(1)}, f32[32,1,16,128]{3,0,2,1:T(8,128)S(1)}, u32[]{:S(2)}, u32[]{:S(2)}) collective-permute-start(f32[32,1,16,128]{3,0,2,1:T(8,128)S(1)} %get-tuple-element.29), channel_id=1, source_target_pairs={{16,0},{32,16},{48,32},{64,48},{80,64},{96,80},{112,96},{17,1},{33... | collective-permute-start | bytes 786440 | tf_op jit(solution)/shard_map/ppermute | solution.py:17
  66.5 11.9 %collective-permute-start.9 = (f32[32,1,16,128]{3,0,2,1:T(8,128)S(1)}, f32[32,1,16,128]{3,0,2,1:T(8,128)S(1)}, u32[]{:S(2)}, u32[]{:S(2)}) collective-permute-start(f32[32,1,16,128]{3,0,2,1:T(8,128)S(1)} %get-tuple-element.28), channel_id=1, source_target_pairs={{0,16},{16,32},{32,48},{48,64},{64,80},{80,96},{96,112},{1,17},{17... | collective-permute-start | bytes 786440 | tf_op jit(solution)/shard_map/ppermute | solution.py:14
  78.4 6.9 %collective-permute-start.10 = (f32[32,18,1,128]{3,0,2,1:T(8,128)S(1)}, f32[32,18,1,128]{3,0,2,1:T(8,128)S(1)}, u32[]{:S(2)}, u32[]{:S(2)}) collective-permute-start(f32[32,18,1,128]{3,0,2,1:T(8,128)S(1)} %get-tuple-element.18), channel_id=1, source_target_pairs={{2,0},{4,2},{6,4},{8,6},{10,8},{12,10},{14,12},{3,1},{5,3},{7,5},{... | collective-permute-start | bytes 884744 | tf_op jit(solution)/shard_map/ppermute | solution.py:17
  79.7 6.8 %collective-permute-start.11 = (f32[32,18,1,128]{3,0,2,1:T(8,128)S(1)}, f32[32,18,1,128]{3,0,2,1:T(8,128)S(1)}, u32[]{:S(2)}, u32[]{:S(2)}) collective-permute-start(f32[32,18,1,128]{3,0,2,1:T(8,128)S(1)} %get-tuple-element.19), channel_id=1, source_target_pairs={{0,2},{2,4},{4,6},{6,8},{8,10},{10,12},{12,14},{1,3},{3,5},{5,7},{... | collective-permute-start | bytes 884744 | tf_op jit(solution)/shard_map/ppermute | solution.py:14
  94.6 8.3 %collective-permute-start.12 = (f32[32,1,16,128]{3,0,2,1:T(8,128)S(1)}, f32[32,1,16,128]{3,0,2,1:T(8,128)S(1)}, u32[]{:S(2)}, u32[]{:S(2)}) collective-permute-start(f32[32,1,16,128]{3,0,2,1:T(8,128)S(1)} %get-tuple-element.27), channel_id=1, source_target_pairs={{16,0},{32,16},{48,32},{64,48},{80,64},{96,80},{112,96},{17,1},{33... | collective-permute-start | bytes 786440 | tf_op jit(solution)/shard_map/ppermute | solution.py:17
  96.5 11.9 %collective-permute-start.13 = (f32[32,1,16,128]{3,0,2,1:T(8,128)S(1)}, f32[32,1,16,128]{3,0,2,1:T(8,128)S(1)}, u32[]{:S(2)}, u32[]{:S(2)}) collective-permute-start(f32[32,1,16,128]{3,0,2,1:T(8,128)S(1)} %get-tuple-element.26), channel_id=1, source_target_pairs={{0,16},{16,32},{32,48},{48,64},{64,80},{80,96},{96,112},{1,17},{17... | collective-permute-start | bytes 786440 | tf_op jit(solution)/shard_map/ppermute | solution.py:14
  108.5 10.2 %collective-permute-start.14 = (f32[32,18,1,128]{3,0,2,1:T(8,128)S(1)}, f32[32,18,1,128]{3,0,2,1:T(8,128)S(1)}, u32[]{:S(2)}, u32[]{:S(2)}) collective-permute-start(f32[32,18,1,128]{3,0,2,1:T(8,128)S(1)} %get-tuple-element.16), channel_id=1, source_target_pairs={{2,0},{4,2},{6,4},{8,6},{10,8},{12,10},{14,12},{3,1},{5,3},{7,5},{... | collective-permute-start | bytes 884744 | tf_op jit(solution)/shard_map/ppermute | solution.py:17
  109.8 10.1 %collective-permute-start.15 = (f32[32,18,1,128]{3,0,2,1:T(8,128)S(1)}, f32[32,18,1,128]{3,0,2,1:T(8,128)S(1)}, u32[]{:S(2)}, u32[]{:S(2)}) collective-permute-start(f32[32,18,1,128]{3,0,2,1:T(8,128)S(1)} %get-tuple-element.17), channel_id=1, source_target_pairs={{0,2},{2,4},{4,6},{6,8},{8,10},{10,12},{12,14},{1,3},{3,5},{5,7},{... | collective-permute-start | bytes 884744 | tf_op jit(solution)/shard_map/ppermute | solution.py:14
  128.0 8.3 %collective-permute-start.16 = (f32[32,1,16,128]{3,0,2,1:T(8,128)S(1)}, f32[32,1,16,128]{3,0,2,1:T(8,128)S(1)}, u32[]{:S(2)}, u32[]{:S(2)}) collective-permute-start(f32[32,1,16,128]{3,0,2,1:T(8,128)S(1)} %get-tuple-element.25), channel_id=1, source_target_pairs={{16,0},{32,16},{48,32},{64,48},{80,64},{96,80},{112,96},{17,1},{33... | collective-permute-start | bytes 786440 | tf_op jit(solution)/shard_map/ppermute | solution.py:17
  129.9 11.9 %collective-permute-start.17 = (f32[32,1,16,128]{3,0,2,1:T(8,128)S(1)}, f32[32,1,16,128]{3,0,2,1:T(8,128)S(1)}, u32[]{:S(2)}, u32[]{:S(2)}) collective-permute-start(f32[32,1,16,128]{3,0,2,1:T(8,128)S(1)} %get-tuple-element.24), channel_id=1, source_target_pairs={{0,16},{16,32},{32,48},{48,64},{64,80},{80,96},{96,112},{1,17},{17... | collective-permute-start | bytes 786440 | tf_op jit(solution)/shard_map/ppermute | solution.py:14
  141.8 9.9 %collective-permute-start.18 = (f32[32,18,1,128]{3,0,2,1:T(8,128)S(1)}, f32[32,18,1,128]{3,0,2,1:T(8,128)S(1)}, u32[]{:S(2)}, u32[]{:S(2)}) collective-permute-start(f32[32,18,1,128]{3,0,2,1:T(8,128)S(1)} %get-tuple-element.14), channel_id=1, source_target_pairs={{2,0},{4,2},{6,4},{8,6},{10,8},{12,10},{14,12},{3,1},{5,3},{7,5},{... | collective-permute-start | bytes 884744 | tf_op jit(solution)/shard_map/ppermute | solution.py:17
  143.1 9.8 %collective-permute-start.19 = (f32[32,18,1,128]{3,0,2,1:T(8,128)S(1)}, f32[32,18,1,128]{3,0,2,1:T(8,128)S(1)}, u32[]{:S(2)}, u32[]{:S(2)}) collective-permute-start(f32[32,18,1,128]{3,0,2,1:T(8,128)S(1)} %get-tuple-element.15), channel_id=1, source_target_pairs={{0,2},{2,4},{4,6},{6,8},{8,10},{10,12},{12,14},{1,3},{3,5},{5,7},{... | collective-permute-start | bytes 884744 | tf_op jit(solution)/shard_map/ppermute | solution.py:14
  164.8 6.8 %copy-start.5 = (bf16[64,16,16,128]{3,2,1,0:T(8,128)(2,1)S(1)}, bf16[64,16,16,128]{3,2,1,0:T(8,128)(2,1)}, u32[]{:S(2)}) copy-start(bf16[64,16,16,128]{3,2,1,0:T(8,128)(2,1)} %param.9) | copy-start | bytes 12582916
  171.6 334.0 %copy-start.4 = (f32[64,32]{0,1:T(8,128)S(1)}, f32[64,32]{0,1:T(8,128)}, u32[]{:S(2)}) copy-start(f32[64,32]{0,1:T(8,128)} %param.11) | copy-start | bytes 24580
  511.1 1.6 copy-start.3
Sparse Core Ops, SparseCore 0:
  164.9 63.2 all-gather.1
where the time goes:
time: 527 us; the launch traced here: 526 us
  blocking collectives  330 us (63%)
  starting transfers between devices  73.6 us (14%)
  other arithmetic  36.9 us (7%)
  local copies, waits for them, and re-layouts  34.4 us (7%)
  waiting for transfers between devices  28.3 us (5%)
  between operations  14.5 us (3%)
  matrix products  7.84 us (1%)
    psum x1, blocking collectives, per_device(): corange_sketch = corange_prev + lax.psum(partial_value, ('sx', 'sy'))  330 us
    ppermute x10, starting transfers between devices, extended(): lax.ppermute(lax.slice_in_dim(block, block.shape[dim] - width, None, axis...  47.4 us
    unnamed x22, local copies, waits for them, and re-layouts  30.2 us
    add x3, other arithmetic, advance(): return center + 0.16 * total  26.5 us
    ppermute x10, starting transfers between devices, extended(): lax.ppermute(lax.slice_in_dim(block, 0, width, axis=dim), axis, backward)  26.1 us
    ppermute x10, waiting for transfers between devices, extended(): lax.ppermute(lax.slice_in_dim(block, block.shape[dim] - width, None, axis...  21.1 us
  transfers between devices with their start and end apart: 21, of which 10 were waited for; matrix products, arithmetic and copies ran while one was open for 4% of the time, Pallas kernels for 0%

commit v1 on v0

v1 whole, which is shorter than its diff:
```python
import functools

import jax
import jax.numpy as jnp
from jax import lax
from jax.experimental import pallas as pl
from jax.experimental.pallas import tpu as pltpu
from jax.sharding import PartitionSpec as P

STEPS = 4
H = STEPS
MESH = pl.DeviceIdType.MESH
F32 = jnp.float32
BF16 = jnp.bfloat16
CHUNK = 2


def kernel(
    u_hbm, k_hbm, omega_ref, psi_hbm, prev_hbm, cprev_ref,
    fin_hbm, range_hbm, cor_ref,
    u_in, k_in, xs, xr, ys, yr, snap, peer, psi, prev, acc, w_ref, red, part, gat1, part2, gat2,
    ua, ub, kk, cx, cy, cz, dd, rout,
    load_sem, aux_sem, xs_sem, xr_sem, ys_sem, yr_sem, ps_sem, pr_sem, fo_sem, ro_sem,
    a1s_sem, a1r_sem, a2s_sem, a2r_sem,
):
    S, X, Y, Z = u_in.shape
    NC = S // CHUNK
    XE = X + 2 * H
    R = psi.shape[0]
    RD = prev.shape[0]
    sx, sy, par = lax.axis_index("sx"), lax.axis_index("sy"), lax.axis_index("par")
    nsx, nsy = gat1.shape[0], gat2.shape[0]
    has = {("sx", 0): sx > 0, ("sx", 1): sx < nsx - 1, ("sy", 0): sy > 0, ("sy", 1): sy < nsy - 1}
    pos = {"sx": sx, "sy": sy}

    def chunk(c):
        return pl.ds(c * CHUNK, CHUNK)

    def load(c):
        return (
            pltpu.make_async_copy(u_hbm.at[chunk(c)], u_in.at[chunk(c)], load_sem.at[0, c]),
            pltpu.make_async_copy(k_hbm.at[chunk(c)], k_in.at[chunk(c)], load_sem.at[1, c]),
        )

    def halo(axis, side, c):
        send, recv, ssem, rsem = (xs, xr, xs_sem, xr_sem) if axis == "sx" else (ys, yr, ys_sem, yr_sem)
        other = jnp.maximum(pos[axis] - 1, 0) if side == 0 else jnp.minimum(pos[axis] + 1, (nsx if axis == "sx" else nsy) - 1)
        return pltpu.make_async_remote_copy(
            send.at[side, chunk(c)], recv.at[1 - side, chunk(c)], ssem.at[side, c], rsem.at[1 - side, c],
            device_id={axis: other}, device_id_type=MESH,
        )

    def halo_recv(axis, side, c):
        send, recv, ssem, rsem = (xs, xr, xs_sem, xr_sem) if axis == "sx" else (ys, yr, ys_sem, yr_sem)
        other = jnp.maximum(pos[axis] - 1, 0) if side == 0 else jnp.minimum(pos[axis] + 1, (nsx if axis == "sx" else nsy) - 1)
        return pltpu.make_async_remote_copy(
            send.at[side, chunk(c)], recv.at[side, chunk(c)], ssem.at[side, c], rsem.at[side, c],
            device_id={axis: other}, device_id_type=MESH,
        )

    def par_copy(c):
        return pltpu.make_async_remote_copy(
            snap.at[chunk(c)], peer.at[chunk(c)], ps_sem.at[c], pr_sem.at[c],
            device_id={"par": 1 - par}, device_id_type=MESH,
        )

    def fin_copy(c):
        return pltpu.make_async_copy(u_in.at[chunk(c)], fin_hbm.at[chunk(c)], fo_sem.at[c])

    @pl.loop(0, NC)
    def _(c):
        for cp in load(c):
            cp.start()

    psi_load = pltpu.make_async_copy(psi_hbm, psi, aux_sem.at[0])
    prev_load = pltpu.make_async_copy(prev_hbm, prev, aux_sem.at[1])
    psi_load.start()
    prev_load.start()

    barrier = pltpu.get_barrier_semaphore()
    for d in range(1, nsx):
        pl.semaphore_signal(barrier, inc=1, device_id={"sx": lax.rem(sx + d, nsx)}, device_id_type=MESH)
    for d in range(1, nsy):
        pl.semaphore_signal(barrier, inc=1, device_id={"sy": lax.rem(sy + d, nsy)}, device_id_type=MESH)
    pl.semaphore_signal(barrier, inc=1, device_id={"par": 1 - par}, device_id_type=MESH)

    for side in (0, 1):
        @pl.when(jnp.logical_not(has["sx", side]))
        def _():
            @pl.loop(0, S)
            def _(s):
                xr[side, s] = jnp.zeros(xr.shape[2:], BF16)

        @pl.when(jnp.logical_not(has["sy", side]))
        def _():
            @pl.loop(0, S)
            def _(s):
                yr[side, s] = jnp.zeros(yr.shape[2:], BF16)

    row8 = lax.broadcasted_iota(jnp.int32, (1, 8, Z), 1)
    low4 = row8 < 4
    yrow = lax.broadcasted_iota(jnp.int32, (1, Y + 2 * H, Z), 1)
    lane = lax.broadcasted_iota(jnp.int32, (1, Y + 2 * H, Z), 2)
    cut = ((yrow == H - 1) & (sy == 0)) | ((yrow == H + Y - 1) & (sy == nsy - 1))
    ymask = jnp.where(cut, 0.0, 1.0).astype(F32)

    pl.semaphore_wait(barrier, nsx + nsy - 1)

    @pl.loop(0, NC)
    def _(c):
        for cp in load(c):
            cp.wait()

        @pl.loop(0, CHUNK)
        def _(j):
            s = c * CHUNK + j
            for side, at in ((0, 0), (1, X - H)):
                xs[side, s, 0:H] = u_in[s, at:at + H].astype(BF16)
                xs[side, s, H:2 * H] = k_in[s, at:at + H].astype(BF16)

        for side in (0, 1):
            @pl.when(has["sx", side])
            def _():
                halo("sx", side, c).start()

    def half(s, x0, n, tile):
        rows = slice(8 * tile, 8 * tile + 8)
        if x0 < H:
            v = xr[0, s].astype(F32)
            return v[0:H, rows], v[H:2 * H, rows]
        if x0 >= H + X:
            v = xr[1, s].astype(F32)
            return v[0:H, rows], v[H:2 * H, rows]
        return u_in[s, x0 - H:x0 - H + n, rows], k_in[s, x0 - H:x0 - H + n, rows]

    groups = [(x0, H) for x0 in range(0, XE, H)]

    def y_edges(c):
        for side in (0, 1):
            @pl.when(has["sx", side])
            def _():
                halo_recv("sx", side, c).wait_recv()

        @pl.loop(0, CHUNK)
        def _(j):
            s = c * CHUNK + j
            for x0, n in groups:
                u0, k0 = half(s, x0, n, 0)
                u1, k1 = half(s, x0, n, 1)
                p = jnp.where(low4, k0, pltpu.roll(u0, 4, 1))
                q = jnp.where(low4, pltpu.roll(u1, 4, 1), k1)
                ys[0, s, x0 // 2:x0 // 2 + n // 2] = p.reshape(n // 2, 16, Z).astype(BF16)
                ys[1, s, x0 // 2:x0 // 2 + n // 2] = q.reshape(n // 2, 16, Z).astype(BF16)

        for side in (0, 1):
            @pl.when(has["sy", side])
            def _():
                halo("sy", side, c).start()

    def zshift(v, by):
        return pltpu.roll(v, by % Z, 2)

    def yshift(v, by):
        return pltpu.roll(v, by % v.shape[1], 1)

    def sample(s):
        for x0, n in groups:
            u0, k0 = half(s, x0, n, 0)
            u1, k1 = half(s, x0, n, 1)
            lo = yr[0, s, x0 // 2:x0 // 2 + n // 2].astype(F32).reshape(n, 8, Z)
            hi = yr[1, s, x0 // 2:x0 // 2 + n // 2].astype(F32).reshape(n, 8, Z)
            a, b = pltpu.roll(u0, 4, 1), pltpu.roll(u1, 4, 1)
            ua[x0:x0 + n, 0:8] = jnp.where(low4, lo, a)
            ua[x0:x0 + n, 8:16] = jnp.where(low4, a, b)
            ua[x0:x0 + n, 16:24] = jnp.where(low4, b, hi)
            a, b = pltpu.roll(k0, 4, 1), pltpu.roll(k1, 4, 1)
            kk[x0:x0 + n, 0:8] = jnp.where(low4, pltpu.roll(lo, 4, 1), a) * 0.08
            kk[x0:x0 + n, 8:16] = jnp.where(low4, a, b) * 0.08
            kk[x0:x0 + n, 16:24] = jnp.where(low4, b, pltpu.roll(hi, 4, 1)) * 0.08

        cx[0:1] = kk[0:1] + kk[1:2]

        def faces(i, _):
            x = pl.ds(1 + 2 * i, 2)
            k = kk[x]
            fx = k + kk[pl.ds(2 + 2 * i, 2)]
            bx = k + kk[pl.ds(2 * i, 2)]
            fy = k + yshift(k, -1)
            by = yshift(fy, 1)
            fz = k + jnp.where(lane < Z - 1, zshift(k, -1), 0.0)
            bz = k + jnp.where(lane > 0, zshift(k, 1), 0.0)
            dd[x] = 1.0 - (((fx + bx) + (fy + by)) + (fz + bz))
            cx[x] = fx
            cy[x] = fy * ymask
            cz[x] = jnp.where(lane < Z - 1, fz, 0.0)
            return 0

        lax.fori_loop(0, (XE - 2) // 2, faces, 0, unroll=True)

        @pl.when(sx == 0)
        def _():
            cx[H - 1:H] = jnp.zeros((1, Y + 2 * H, Z), F32)

        @pl.when(sx == nsx - 1)
        def _():
            cx[H + X - 1:H + X] = jnp.zeros((1, Y + 2 * H, Z), F32)

        def stencil(src, x0):
            x = pl.ds(x0, 2)
            u = src[x]
            y_c, z_c = cy[x], cz[x]
            out = dd[x] * u
            out += cx[x] * src[pl.ds(x0 + 1, 2)] + cx[pl.ds(x0 - 1, 2)] * src[pl.ds(x0 - 1, 2)]
            out += y_c * yshift(u, -1) + yshift(y_c * u, 1)
            out += z_c * zshift(u, -1) + zshift(z_c * u, 1)
            return out

        src, dst = ua, ub
        for step in range(STEPS - 1):
            first = 1 + step

            def advance(i, _, src=src, dst=dst, first=first):
                dst[pl.ds(first + 2 * i, 2)] = stencil(src, first + 2 * i)
                return 0

            lax.fori_loop(0, (XE - 2 * first) // 2, advance, 0, unroll=True)
            src, dst = dst, src

        def last(i, _, src=src):
            v = stencil(src, H + 2 * i)
            v0, v1, v2 = (pltpu.roll(v[:, 8 * t:8 * t + 8], 4, 1) for t in range(3))
            a, b = jnp.where(low4, v0, v1), jnp.where(low4, v1, v2)
            o = jnp.concatenate([a, b], axis=1)
            u_in[s, pl.ds(2 * i, 2)] = o
            snap[s, pl.ds(2 * i, 2)] = o.astype(BF16)
            return 0

        lax.fori_loop(0, X // 2, last, 0, unroll=True)

    y_edges(0)
    y_edges(1)

    i_r = lax.broadcasted_iota(jnp.int32, (RD * Y, R), 0) // Y
    i_j = lax.broadcasted_iota(jnp.int32, (RD * Y, R), 1)
    pick = jnp.where(i_j == i_r + par * RD, 1.0, 0.0).astype(BF16)
    cols = lax.dot_general(pick, omega_ref[...], (((1,), (1,)), ((), ())), preferred_element_type=F32).astype(BF16)
    total = omega_ref.shape[0]
    WB = 256

    @pl.loop(0, total * Y // WB)
    def _(b):
        e_s = lax.broadcasted_iota(jnp.int32, (total, WB), 0)
        e_c = lax.broadcasted_iota(jnp.int32, (total, WB), 1) + b * WB
        spread = jnp.where(e_s == lax.rem(e_c // Y + par * S, total), 1.0, 0.0).astype(BF16)
        wide = jnp.dot(cols, spread, preferred_element_type=F32)
        w_r = lax.rem(lax.broadcasted_iota(jnp.int32, (RD * Y, WB), 0), Y)
        w_c = lax.rem(lax.broadcasted_iota(jnp.int32, (RD * Y, WB), 1), Y)
        w_ref[:, pl.ds(pl.multiple_of(b * WB, WB), WB)] = jnp.where(w_r == w_c, wide, 0.0).astype(BF16)

    @pl.loop(0, NC)
    def _(c):
        @pl.when(c + 2 < NC)
        def _():
            y_edges(c + 2)

        for side in (0, 1):
            @pl.when(has["sy", side])
            def _():
                halo_recv("sy", side, c).wait_recv()

        @pl.loop(0, CHUNK)
        def _(j):
            sample(c * CHUNK + j)

        par_copy(c).start()
        fin_copy(c).start()

    psi_load.wait()
    SB, RB = 16, 16

    @pl.loop(0, (R // RB) * (S // SB))
    def _(b):
        rb, sb = b // (S // SB), lax.rem(b, S // SB)
        val = None
        for x in range(0, X, 2):
            left = jnp.concatenate([psi[pl.ds(rb * RB, RB), x + d].reshape(RB * Y, Z) for d in range(2)], axis=1)
            right = jnp.concatenate([snap[pl.ds(sb * SB, SB), x + d].reshape(SB * Y, Z) for d in range(2)], axis=1)
            term = lax.dot_general(left, right, (((1,), (1,)), ((), ())), preferred_element_type=F32)
            val = term if val is None else val + term
        w_r = lax.rem(lax.broadcasted_iota(jnp.int32, (RB * Y, SB * Y), 0), Y)
        w_c = lax.rem(lax.broadcasted_iota(jnp.int32, (RB * Y, SB * Y), 1), Y)
        val = jnp.where(w_r == w_c, val, 0.0).reshape(RB, Y, SB * Y)
        red[sb, pl.ds(rb * RB, RB)] = jnp.sum(val, axis=1)

    Q = Z // S
    RQ = R // Q
    dense = jnp.zeros((RQ, Z), F32)
    for q in range(Q):
        for sb in range(S // SB):
            g_c = lax.broadcasted_iota(jnp.int32, (SB * Y, Z), 0) // Y + sb * SB + q * S
            g_l = lax.broadcasted_iota(jnp.int32, (SB * Y, Z), 1)
            group = jnp.where(g_c == g_l, 1.0, 0.0).astype(F32)
            dense += jnp.dot(red[sb, q * RQ:(q + 1) * RQ], group, preferred_element_type=F32, precision=lax.Precision.HIGHEST)
    part[...] = dense

    def gather(axis, d, src, dst, ssem, rsem):
        n = dst.shape[0]
        to = lax.rem(pos[axis] + d, n)
        frm = lax.rem(pos[axis] + n - d, n)
        out = pltpu.make_async_remote_copy(
            src, dst.at[pos[axis]], ssem.at[d], rsem.at[d], device_id={axis: to}, device_id_type=MESH)
        inn = pltpu.make_async_remote_copy(
            src, dst.at[frm], ssem.at[d], rsem.at[d], device_id={axis: to}, device_id_type=MESH)
        return out, inn

    for d in range(1, nsx):
        gather("sx", d, part, gat1, a1s_sem, a1r_sem)[0].start()

    prev_load.wait()

    def range_part(x0, weights, source, lo, n):
        right = jnp.concatenate([source[lo:lo + n, x0 + d].reshape(n * Y, Z) for d in range(2)], axis=1)
        return jnp.dot(weights, right, preferred_element_type=F32)

    for x0 in range(0, X, 2):
        t = range_part(x0, w_ref[:, 0:S * Y], snap, 0, S)
        for d in range(2):
            acc[x0 + d] = prev[:, x0 + d].reshape(RD * Y, Z).astype(F32) + t[:, d * Z:(d + 1) * Z]

    gat1[pl.ds(sx, 1)] = part[...][None]
    for d in range(1, nsx):
        out, inn = gather("sx", d, part, gat1, a1s_sem, a1r_sem)
        out.wait_send()
        inn.wait_recv()
    tot = gat1[0]
    for i in range(1, nsx):
        tot += gat1[i]
    part2[...] = tot
    for d in range(1, nsy):
        gather("sy", d, part2, gat2, a2s_sem, a2r_sem)[0].start()

    HALF = S // 2
    for c in range(NC // 2):
        par_copy(c).wait_recv()
    for x0 in range(0, X, 2):
        t = range_part(x0, w_ref[:, S * Y:(S + HALF) * Y], peer, 0, HALF)
        for d in range(2):
            acc[x0 + d] = acc[x0 + d] + t[:, d * Z:(d + 1) * Z]

    gat2[pl.ds(sy, 1)] = part2[...][None]
    for d in range(1, nsy):
        out, inn = gather("sy", d, part2, gat2, a2s_sem, a2r_sem)
        out.wait_send()
        inn.wait_recv()
    tot = gat2[0]
    for i in range(1, nsy):
        tot += gat2[i]
    for q in range(Q):
        cor_ref[q * RQ:(q + 1) * RQ] = cprev_ref[q * RQ:(q + 1) * RQ] + tot[:, q * S:(q + 1) * S]

    for c in range(NC // 2, NC):
        par_copy(c).wait_recv()

    def range_out(x0):
        return pltpu.make_async_copy(rout.at[:, pl.ds(x0, 2)], range_hbm.at[:, pl.ds(x0, 2)], ro_sem.at[x0 // 2])

    for x0 in range(0, X, 2):
        t = range_part(x0, w_ref[:, (S + HALF) * Y:2 * S * Y], peer, HALF, HALF)
        for d in range(2):
            v = acc[x0 + d] + t[:, d * Z:(d + 1) * Z]
            rout[:, x0 + d] = v.astype(BF16).reshape(RD, Y, Z)
        range_out(x0).start()

    @pl.loop(0, NC)
    def _(c):
        for side in (0, 1):
            for axis in ("sx", "sy"):
                @pl.when(has[axis, side])
                def _():
                    halo(axis, side, c).wait_send()
        par_copy(c).wait_send()
        fin_copy(c).wait()

    for x0 in range(0, X, 2):
        range_out(x0).wait()


def per_device(sizes, initial_state, conductivity, omega, psi, range_prev, corange_prev):
    S, X, Y, Z = initial_state.shape
    R, RD = psi.shape[0], range_prev.shape[0]
    nsx, nsy = sizes
    NC = S // CHUNK
    E = (X + 2 * H, Y + 2 * H, Z)
    dma = pltpu.SemaphoreType.DMA
    scratch = [
        pltpu.VMEM((S, X, Y, Z), F32),
        pltpu.VMEM((S, X, Y, Z), F32),
        pltpu.VMEM((2, S, 2 * H, Y, Z), BF16),
        pltpu.VMEM((2, S, 2 * H, Y, Z), BF16),
        pltpu.VMEM((2, S, E[0] // 2, 16, Z), BF16),
        pltpu.VMEM((2, S, E[0] // 2, 16, Z), BF16),
        pltpu.VMEM((S, X, Y, Z), BF16),
        pltpu.VMEM((S, X, Y, Z), BF16),
        pltpu.VMEM((R, X, Y, Z), BF16),
        pltpu.VMEM((RD, X, Y, Z), BF16),
        pltpu.VMEM((X, RD * Y, Z), F32),
        pltpu.VMEM((RD * Y, 2 * S * Y), BF16),
        pltpu.VMEM((S // 16, R, 16 * Y), F32),
        pltpu.VMEM((R * S // Z, Z), F32),
        pltpu.VMEM((nsx, R * S // Z, Z), F32),
        pltpu.VMEM((R * S // Z, Z), F32),
        pltpu.VMEM((nsy, R * S // Z, Z), F32),
    ] + [pltpu.VMEM(E, F32)] * 7 + [
        pltpu.VMEM((RD, X, Y, Z), BF16),
        dma((2, NC)), dma((2,)), dma((2, NC)), dma((2, NC)), dma((2, NC)), dma((2, NC)),
        dma((NC,)), dma((NC,)), dma((NC,)), dma((X // 2,)),
        dma((nsx,)), dma((nsx,)), dma((nsy,)), dma((nsy,)),
    ]
    any_ = pl.BlockSpec(memory_space=pl.ANY)
    vmem = pl.BlockSpec(memory_space=pltpu.VMEM)
    return pl.pallas_call(
        kernel,
        out_shape=(
            jax.ShapeDtypeStruct(initial_state.shape, F32),
            jax.ShapeDtypeStruct(range_prev.shape, BF16),
            jax.ShapeDtypeStruct(corange_prev.shape, F32),
        ),
        in_specs=[any_, any_, vmem, any_, any_, vmem],
        out_specs=(any_, any_, vmem),
        scratch_shapes=scratch,
        compiler_params=pltpu.CompilerParams(
            collective_id=0, has_side_effects=True, vmem_limit_bytes=60 * 2**20
        ),
    )(initial_state, conductivity, omega, psi, range_prev, corange_prev)


def solution(mesh):
    in_specs = (
        P("par", "sx", "sy", None),
        P("par", "sx", "sy", None),
        P(),
        P(None, "sx", "sy", None),
        P("par", "sx", "sy", None),
        P(None, "par"),
    )
    out_specs = (P("par", "sx", "sy", None), P("par", "sx", "sy", None), P(None, "par"))
    sizes = (mesh.shape["sx"], mesh.shape["sy"])
    return jax.shard_map(
        functools.partial(per_device, sizes), mesh=mesh, in_specs=in_specs, out_specs=out_specs, check_vma=False
    )
```

time: 527 us -> 96.7 us (0.18)
  the two profiles are of different devices: /device:TPU:24 before, /device:TPU:1 now
where the time goes in v1:
time: 96.7 us; the launch traced here: 96.4 us
  Pallas kernels  86.8 us (90%)
  local copies, waits for them, and re-layouts  8.98 us (9%)
    pallas_call x1, Pallas kernels, per_device(): pl.pallas_call(kernel, out_shape=(jax.ShapeDtypeStruct(initial_state.shap...  86.8 us
    unnamed x5, local copies, waits for them, and re-layouts  7.54 us

profile of v1, /device:TPU:1, one launch (start us, length us, event | category | flops | bytes accessed | tf_op | source)
XLA Modules:
  0.0 96.4 jit_solution(12870709914875208572)
XLA Ops:
  0.6 1.4 %copy.9.cprev_ref = f32[64,32]{1,0:T(8,128)} copy(f32[64,32]{0,1:T(8,128)} %param.11) | data formatting | bytes 16384 | tf_op args[5]
  2.0 86.8 %shard_map.85 = (f32[32,16,16,128]{3,2,1,0:T(8,128)}, bf16[32,16,16,128]{3,2,1,0:T(8,128)(2,1)}, f32[64,32]{1,0:T(8,128)}) custom-call(f32[32,16,16,128]{3,2,1,0:T(8,128)} %u_hbm.1, f32[32,16,16,128]{3,2,1,0:T(8,128)} %k_hbm.1, bf16[64,64]{1,0:T(8,128)(2,1)} %omega_ref.1, bf16[64,16,16,128]{3,2,1,0:T(8,128)(2,1)} %psi_hbm.1, ...), custom_call_target="tpu_custom_call" | custom-call | tf_op jit(solution)/shard_map/pallas_call | solution.py:421
  88.9 1.4 %copy.10 = f32[64,32]{0,1:T(8,128)} copy(f32[64,32]{1,0:T(8,128)} %get-tuple-element.5) | data formatting | bytes 16384 | tf_op jit(solution)/shard_map/pallas_call | solution.py:421
  90.3 0.0 copy-start
  90.3 4.8 %copy.13 = f32[32,16,16,128]{3,2,1,0:T(8,128)} copy(f32[32,16,16,128]{3,2,1,0:T(8,128)} %get-tuple-element.9) | data formatting | bytes 8388608
  95.1 0.0 copy-done
  95.1 1.3 %copy.14 = bf16[32,16,16,128]{3,2,1,0:T(8,128)(2,1)} copy(bf16[32,16,16,128]{3,2,1,0:T(8,128)(2,1)S(1)} %copy-done) | data formatting | bytes 4194304
Async XLA Ops:
  90.3 4.8 %copy-start = (bf16[32,16,16,128]{3,2,1,0:T(8,128)(2,1)S(1)}, bf16[32,16,16,128]{3,2,1,0:T(8,128)(2,1)}, u32[]{:S(2)}) copy-start(bf16[32,16,16,128]{3,2,1,0:T(8,128)(2,1)} %get-tuple-element.10) | copy-start | bytes 6291460

commit v2 on v1

--- a/solution.py
+++ b/solution.py
@@ -13,14 +13,17 @@
 F32 = jnp.float32
 BF16 = jnp.bfloat16
 CHUNK = 2
+AHEAD = 16
+HELD = 4
+VMEM_MIB = 44
 
 
 def kernel(
     u_hbm, k_hbm, omega_ref, psi_hbm, prev_hbm, cprev_ref,
-    fin_hbm, range_hbm, cor_ref,
-    u_in, k_in, xs, xr, ys, yr, snap, peer, psi, prev, acc, w_ref, red, part, gat1, part2, gat2,
-    ua, ub, kk, cx, cy, cz, dd, rout,
-    load_sem, aux_sem, xs_sem, xr_sem, ys_sem, yr_sem, ps_sem, pr_sem, fo_sem, ro_sem,
+    u_in, rout, cor_ref,
+    k_in, xs, xr, rly, ys, yr, snap, peer, psi, prev, acc, w_ref, red, part, gat1, part2, gat2,
+    ua, ub, kk, cx, cy, cz, dd,
+    load_sem, aux_sem, xs_sem, xr_sem, ry_sem, rf_sem, ys_sem, yr_sem, ps_sem, pr_sem,
     a1s_sem, a1r_sem, a2s_sem, a2r_sem,
 ):
     S, X, Y, Z = u_in.shape
@@ -42,30 +45,64 @@
             pltpu.make_async_copy(k_hbm.at[chunk(c)], k_in.at[chunk(c)], load_sem.at[1, c]),
         )
 
+    XW = nsx // 2
+
+    def remote(src, dst, ssem, rsem, axis, other):
+        return pltpu.make_async_remote_copy(src, dst, ssem, rsem, device_id={axis: other}, device_id_type=MESH)
+
+    def beside(axis, side):
+        n = nsx if axis == "sx" else nsy
+        return jnp.maximum(pos[axis] - 1, 0) if side == 0 else jnp.minimum(pos[axis] + 1, n - 1)
+
     def halo(axis, side, c):
         send, recv, ssem, rsem = (xs, xr, xs_sem, xr_sem) if axis == "sx" else (ys, yr, ys_sem, yr_sem)
-        other = jnp.maximum(pos[axis] - 1, 0) if side == 0 else jnp.minimum(pos[axis] + 1, (nsx if axis == "sx" else nsy) - 1)
-        return pltpu.make_async_remote_copy(
-            send.at[side, chunk(c)], recv.at[1 - side, chunk(c)], ssem.at[side, c], rsem.at[1 - side, c],
-            device_id={axis: other}, device_id_type=MESH,
-        )
+        return remote(send.at[side, chunk(c)], recv.at[1 - side, chunk(c)], ssem.at[side, c], rsem.at[1 - side, c],
+                      axis, beside(axis, side))
 
     def halo_recv(axis, side, c):
         send, recv, ssem, rsem = (xs, xr, xs_sem, xr_sem) if axis == "sx" else (ys, yr, ys_sem, yr_sem)
-        other = jnp.maximum(pos[axis] - 1, 0) if side == 0 else jnp.minimum(pos[axis] + 1, (nsx if axis == "sx" else nsy) - 1)
-        return pltpu.make_async_remote_copy(
-            send.at[side, chunk(c)], recv.at[side, chunk(c)], ssem.at[side, c], rsem.at[side, c],
-            device_id={axis: other}, device_id_type=MESH,
-        )
+        return remote(send.at[side, chunk(c)], recv.at[side, chunk(c)], ssem.at[side, c], rsem.at[side, c],
+                      axis, beside(axis, side))
+
+    def detour(side, c):
+        q = lax.rem(c, 2) * (XW - 1)
+        at_seam = (sx == XW - 1) if side == 1 else (sx == XW)
+        via = XW + q if side == 1 else XW - 1 - q
+        return at_seam & (q != 0), via, c // 2
+
+    def to_relay(side, c):
+        _, via, m = detour(side, c)
+        return remote(xs.at[side, chunk(c)], rly.at[m], xs_sem.at[side, c], ry_sem.at[m], "sx", via)
+
+    def relay(c):
+        q = lax.rem(c, 2) * (XW - 1)
+        m = c // 2
+        for side in (0, 1):
+            mine = ((sx == XW + q) if side == 1 else (sx == XW - 1 - q)) & (q != 0)
+
+            @pl.when(mine & (c < NC))
+            def _():
+                dest = XW if side == 1 else XW - 1
+                cp = remote(rly.at[m], xr.at[1 - side, chunk(c)], rf_sem.at[m], xr_sem.at[1 - side, c], "sx", dest)
+                remote(rly.at[m], rly.at[m], rf_sem.at[m], ry_sem.at[m], "sx", dest).wait_recv()
+                cp.start()
+
+    def relay_done(c):
+        q = lax.rem(c, 2) * (XW - 1)
+        m = c // 2
+        for side in (0, 1):
+            mine = ((sx == XW + q) if side == 1 else (sx == XW - 1 - q)) & (q != 0)
+
+            @pl.when(mine)
+            def _():
+                dest = XW if side == 1 else XW - 1
+                remote(rly.at[m], xr.at[1 - side, chunk(c)], rf_sem.at[m], xr_sem.at[1 - side, c], "sx", dest).wait_send()
 
     def par_copy(c):
         return pltpu.make_async_remote_copy(
             snap.at[chunk(c)], peer.at[chunk(c)], ps_sem.at[c], pr_sem.at[c],
             device_id={"par": 1 - par}, device_id_type=MESH,
         )
-
-    def fin_copy(c):
-        return pltpu.make_async_copy(u_in.at[chunk(c)], fin_hbm.at[chunk(c)], fo_sem.at[c])
 
     @pl.loop(0, NC)
     def _(c):
@@ -106,8 +143,7 @@
 
     pl.semaphore_wait(barrier, nsx + nsy - 1)
 
-    @pl.loop(0, NC)
-    def _(c):
+    def x_edges(c):
         for cp in load(c):
             cp.wait()
 
@@ -119,9 +155,19 @@
                 xs[side, s, H:2 * H] = k_in[s, at:at + H].astype(BF16)
 
         for side in (0, 1):
-            @pl.when(has["sx", side])
+            turn = detour(side, c)[0]
+
+            @pl.when(has["sx", side] & turn)
+            def _():
+                to_relay(side, c).start()
+
+            @pl.when(has["sx", side] & jnp.logical_not(turn))
             def _():
                 halo("sx", side, c).start()
+
+    @pl.loop(0, AHEAD)
+    def _(c):
+        x_edges(c)
 
     def half(s, x0, n, tile):
         rows = slice(8 * tile, 8 * tile + 8)
@@ -238,6 +284,8 @@
         lax.fori_loop(0, X // 2, last, 0, unroll=True)
 
     y_edges(0)
+    relay(jnp.int32(1))
+    relay(jnp.int32(2))
     y_edges(1)
 
     i_r = lax.broadcasted_iota(jnp.int32, (RD * Y, R), 0) // Y
@@ -257,8 +305,41 @@
         w_c = lax.rem(lax.broadcasted_iota(jnp.int32, (RD * Y, WB), 1), Y)
         w_ref[:, pl.ds(pl.multiple_of(b * WB, WB), WB)] = jnp.where(w_r == w_c, wide, 0.0).astype(BF16)
 
+    SB, RB = 16, 16
+
+    def corange(sb):
+        @pl.loop(0, R // RB)
+        def _(rb):
+            val = None
+            for x in range(0, X, 2):
+                left = jnp.concatenate([psi[pl.ds(rb * RB, RB), x + d].reshape(RB * Y, Z) for d in range(2)], axis=1)
+                right = jnp.concatenate([snap[pl.ds(sb * SB, SB), x + d].reshape(SB * Y, Z) for d in range(2)], axis=1)
+                term = lax.dot_general(left, right, (((1,), (1,)), ((), ())), preferred_element_type=F32)
+                val = term if val is None else val + term
+            w_r = lax.rem(lax.broadcasted_iota(jnp.int32, (RB * Y, SB * Y), 0), Y)
+            w_c = lax.rem(lax.broadcasted_iota(jnp.int32, (RB * Y, SB * Y), 1), Y)
+            val = jnp.where(w_r == w_c, val, 0.0).reshape(RB, Y, SB * Y)
+            red[sb, pl.ds(rb * RB, RB)] = jnp.sum(val, axis=1)
+
+    psi_load.wait()
+
     @pl.loop(0, NC)
     def _(c):
+        for sb in range(S // SB - 1):
+            @pl.when(c == (sb + 1) * SB // CHUNK)
+            def _():
+                corange(sb)
+
+        @pl.when(c + AHEAD < NC)
+        def _():
+            x_edges(c + AHEAD)
+
+        upto = jnp.minimum(2 * c + 4, c + 8)
+
+        @pl.loop(jnp.minimum(2 * c + 2, c + 8 - 1) + 1, upto + 1)
+        def _(i):
+            relay(i)
+
         @pl.when(c + 2 < NC)
         def _():
             y_edges(c + 2)
@@ -272,49 +353,33 @@
         def _(j):
             sample(c * CHUNK + j)
 
-        par_copy(c).start()
-        fin_copy(c).start()
-
-    psi_load.wait()
-    SB, RB = 16, 16
-
-    @pl.loop(0, (R // RB) * (S // SB))
-    def _(b):
-        rb, sb = b // (S // SB), lax.rem(b, S // SB)
-        val = None
-        for x in range(0, X, 2):
-            left = jnp.concatenate([psi[pl.ds(rb * RB, RB), x + d].reshape(RB * Y, Z) for d in range(2)], axis=1)
-            right = jnp.concatenate([snap[pl.ds(sb * SB, SB), x + d].reshape(SB * Y, Z) for d in range(2)], axis=1)
-            term = lax.dot_general(left, right, (((1,), (1,)), ((), ())), preferred_element_type=F32)
-            val = term if val is None else val + term
-        w_r = lax.rem(lax.broadcasted_iota(jnp.int32, (RB * Y, SB * Y), 0), Y)
-        w_c = lax.rem(lax.broadcasted_iota(jnp.int32, (RB * Y, SB * Y), 1), Y)
-        val = jnp.where(w_r == w_c, val, 0.0).reshape(RB, Y, SB * Y)
-        red[sb, pl.ds(rb * RB, RB)] = jnp.sum(val, axis=1)
-
-    Q = Z // S
-    RQ = R // Q
-    dense = jnp.zeros((RQ, Z), F32)
-    for q in range(Q):
-        for sb in range(S // SB):
-            g_c = lax.broadcasted_iota(jnp.int32, (SB * Y, Z), 0) // Y + sb * SB + q * S
-            g_l = lax.broadcasted_iota(jnp.int32, (SB * Y, Z), 1)
-            group = jnp.where(g_c == g_l, 1.0, 0.0).astype(F32)
-            dense += jnp.dot(red[sb, q * RQ:(q + 1) * RQ], group, preferred_element_type=F32, precision=lax.Precision.HIGHEST)
-    part[...] = dense
+        @pl.when(c < NC - HELD)
+        def _():
+            par_copy(c).start()
+
+    corange(S // SB - 1)
+
+    g_r = lax.broadcasted_iota(jnp.int32, (SB, SB * Y), 0)
+    g_c = lax.broadcasted_iota(jnp.int32, (SB, SB * Y), 1) // Y
+    group = jnp.where(g_r == g_c, 1.0, 0.0).astype(F32)
+    part[...] = jnp.concatenate([
+        lax.dot_general(group, red[q], (((1,), (1,)), ((), ())), preferred_element_type=F32, precision=lax.Precision.HIGHEST)
+        for q in range(S // SB)], axis=1)
 
     def gather(axis, d, src, dst, ssem, rsem):
         n = dst.shape[0]
-        to = lax.rem(pos[axis] + d, n)
-        frm = lax.rem(pos[axis] + n - d, n)
-        out = pltpu.make_async_remote_copy(
-            src, dst.at[pos[axis]], ssem.at[d], rsem.at[d], device_id={axis: to}, device_id_type=MESH)
-        inn = pltpu.make_async_remote_copy(
-            src, dst.at[frm], ssem.at[d], rsem.at[d], device_id={axis: to}, device_id_type=MESH)
-        return out, inn
+        return remote(src, dst.at[pos[axis]], ssem.at[d], rsem.at[d], axis, lax.rem(pos[axis] + d, n))
+
+    def gather_recv(axis, d, src, dst, ssem, rsem):
+        n = dst.shape[0]
+        return remote(src, dst.at[lax.rem(pos[axis] + n - d, n)], ssem.at[d], rsem.at[d], axis, lax.rem(pos[axis] + d, n))
 
     for d in range(1, nsx):
-        gather("sx", d, part, gat1, a1s_sem, a1r_sem)[0].start()
+        gather("sx", d, part, gat1, a1s_sem, a1r_sem).start()
+
+    @pl.loop(NC - HELD, NC)
+    def _(c):
+        par_copy(c).start()
 
     prev_load.wait()
 
@@ -329,15 +394,14 @@
 
     gat1[pl.ds(sx, 1)] = part[...][None]
     for d in range(1, nsx):
-        out, inn = gather("sx", d, part, gat1, a1s_sem, a1r_sem)
-        out.wait_send()
-        inn.wait_recv()
+        gather("sx", d, part, gat1, a1s_sem, a1r_sem).wait_send()
+        gather_recv("sx", d, part, gat1, a1s_sem, a1r_sem).wait_recv()
     tot = gat1[0]
     for i in range(1, nsx):
         tot += gat1[i]
     part2[...] = tot
     for d in range(1, nsy):
-        gather("sy", d, part2, gat2, a2s_sem, a2r_sem)[0].start()
+        gather("sy", d, part2, gat2, a2s_sem, a2r_sem).start()
 
     HALF = S // 2
     for c in range(NC // 2):
@@ -349,27 +413,22 @@
 
     gat2[pl.ds(sy, 1)] = part2[...][None]
     for d in range(1, nsy):
-        out, inn = gather("sy", d, part2, gat2, a2s_sem, a2r_sem)
-        out.wait_send()
-        inn.wait_recv()
+        gather("sy", d, part2, gat2, a2s_sem, a2r_sem).wait_send()
+        gather_recv("sy", d, part2, gat2, a2s_sem, a2r_sem).wait_recv()
     tot = gat2[0]
     for i in range(1, nsy):
         tot += gat2[i]
-    for q in range(Q):
-        cor_ref[q * RQ:(q + 1) * RQ] = cprev_ref[q * RQ:(q + 1) * RQ] + tot[:, q * S:(q + 1) * S]
+    for q in range(S // SB):
+        cor_ref[q * SB:(q + 1) * SB] = cprev_ref[q * SB:(q + 1) * SB] + tot[:, q * R:(q + 1) * R]
 
     for c in range(NC // 2, NC):
         par_copy(c).wait_recv()
-
-    def range_out(x0):
-        return pltpu.make_async_copy(rout.at[:, pl.ds(x0, 2)], range_hbm.at[:, pl.ds(x0, 2)], ro_sem.at[x0 // 2])
 
     for x0 in range(0, X, 2):
         t = range_part(x0, w_ref[:, (S + HALF) * Y:2 * S * Y], peer, HALF, HALF)
         for d in range(2):
             v = acc[x0 + d] + t[:, d * Z:(d + 1) * Z]
             rout[:, x0 + d] = v.astype(BF16).reshape(RD, Y, Z)
-        range_out(x0).start()
 
     @pl.loop(0, NC)
     def _(c):
@@ -378,11 +437,20 @@
                 @pl.when(has[axis, side])
                 def _():
                     halo(axis, side, c).wait_send()
+        relay_done(c)
         par_copy(c).wait_send()
-        fin_copy(c).wait()
-
-    for x0 in range(0, X, 2):
-        range_out(x0).wait()
+
+
+def store(fin_ref, rng_ref, fin_hbm, rng_hbm, sem):
+    parts = 4
+    copies = []
+    for i, (src, dst) in enumerate(((fin_ref, fin_hbm), (rng_ref, rng_hbm))):
+        n = src.shape[0] // parts
+        copies += [pltpu.make_async_copy(src.at[pl.ds(p * n, n)], dst.at[pl.ds(p * n, n)], sem.at[i, p]) for p in range(parts)]
+    for cp in copies:
+        cp.start()
+    for cp in copies:
+        cp.wait()
 
 
 def per_device(sizes, initial_state, conductivity, omega, psi, range_prev, corange_prev):
@@ -394,9 +462,9 @@
     dma = pltpu.SemaphoreType.DMA
     scratch = [
         pltpu.VMEM((S, X, Y, Z), F32),
-        pltpu.VMEM((S, X, Y, Z), F32),
         pltpu.VMEM((2, S, 2 * H, Y, Z), BF16),
         pltpu.VMEM((2, S, 2 * H, Y, Z), BF16),
+        pltpu.VMEM((NC // 2, CHUNK, 2 * H, Y, Z), BF16),
         pltpu.VMEM((2, S, E[0] // 2, 16, Z), BF16),
         pltpu.VMEM((2, S, E[0] // 2, 16, Z), BF16),
         pltpu.VMEM((S, X, Y, Z), BF16),
@@ -411,27 +479,39 @@
         pltpu.VMEM((R * S // Z, Z), F32),
         pltpu.VMEM((nsy, R * S // Z, Z), F32),
     ] + [pltpu.VMEM(E, F32)] * 7 + [
-        pltpu.VMEM((RD, X, Y, Z), BF16),
-        dma((2, NC)), dma((2,)), dma((2, NC)), dma((2, NC)), dma((2, NC)), dma((2, NC)),
-        dma((NC,)), dma((NC,)), dma((NC,)), dma((X // 2,)),
+        dma((2, NC)), dma((2,)), dma((2, NC)), dma((2, NC)), dma((NC // 2,)), dma((NC // 2,)),
+        dma((2, NC)), dma((2, NC)), dma((NC,)), dma((NC,)),
         dma((nsx,)), dma((nsx,)), dma((nsy,)), dma((nsy,)),
     ]
     any_ = pl.BlockSpec(memory_space=pl.ANY)
+    hbm = pl.BlockSpec(memory_space=pltpu.HBM)
     vmem = pl.BlockSpec(memory_space=pltpu.VMEM)
-    return pl.pallas_call(
+    final, sketch, corange = pl.pallas_call(
         kernel,
         out_shape=(
             jax.ShapeDtypeStruct(initial_state.shape, F32),
             jax.ShapeDtypeStruct(range_prev.shape, BF16),
-            jax.ShapeDtypeStruct(corange_prev.shape, F32),
+            jax.ShapeDtypeStruct(corange_prev.shape[::-1], F32),
         ),
-        in_specs=[any_, any_, vmem, any_, any_, vmem],
-        out_specs=(any_, any_, vmem),
+        in_specs=[hbm, hbm, vmem, hbm, hbm, vmem],
+        out_specs=(vmem, vmem, vmem),
         scratch_shapes=scratch,
         compiler_params=pltpu.CompilerParams(
-            collective_id=0, has_side_effects=True, vmem_limit_bytes=60 * 2**20
+            collective_id=0, has_side_effects=True, vmem_limit_bytes=VMEM_MIB * 2**20
         ),
-    )(initial_state, conductivity, omega, psi, range_prev, corange_prev)
+    )(initial_state, conductivity, omega, psi, range_prev, corange_prev.T)
+    final, sketch = pl.pallas_call(
+        store,
+        out_shape=(
+            jax.ShapeDtypeStruct(initial_state.shape, F32),
+            jax.ShapeDtypeStruct(range_prev.shape, BF16),
+        ),
+        in_specs=[vmem, vmem],
+        out_specs=(any_, any_),
+        scratch_shapes=[dma((2, 4))],
+        compiler_params=pltpu.CompilerParams(vmem_limit_bytes=8 * 2**20),
+    )(final, sketch)
+    return final, sketch, corange.T
 
 
 def solution(mesh):

time: 96.7 us -> 77.6 us (0.80)
  Pallas kernels: 86.8 us -> 73 us
  local copies, waits for them, and re-layouts: 8.98 us -> 3.63 us
    pallas_call x1, Pallas kernels: 86.8 us -> 70.3 us  [per_device(): pl.pallas_call(kernel, out_shape=(jax.ShapeDtypeStruct(initial_state.shap...]
    unnamed x5 -> x7, local copies, waits for them, and re-layouts: 7.54 us -> 3.63 us
    pallas_call x0 -> x1, Pallas kernels: none -> 2.72 us  [per_device(): pl.pallas_call(store, out_shape=(jax.ShapeDtypeStruct(initial_state.shape...]
    pallas_call x1 -> x0, local copies, waits for them, and re-layouts: 1.44 us -> none  [per_device(): pl.pallas_call(kernel, out_shape=(jax.ShapeDtypeStruct(initial_state.shap...]
where the time goes in v2:
time: 77.6 us; the launch traced here: 77.3 us
  Pallas kernels  73 us (94%)
  local copies, waits for them, and re-layouts  3.63 us (5%)
    pallas_call x1, Pallas kernels, per_device(): pl.pallas_call(kernel, out_shape=(jax.ShapeDtypeStruct(initial_state.shap...  70.3 us
    unnamed x7, local copies, waits for them, and re-layouts  3.63 us
    pallas_call x1, Pallas kernels, per_device(): pl.pallas_call(store, out_shape=(jax.ShapeDtypeStruct(initial_state.shape...  2.72 us

profile of v2, /device:TPU:1, one launch (start us, length us, event | category | flops | bytes accessed | tf_op | source)
XLA Modules:
  0.0 77.3 jit_solution(17178370996407315298)
XLA Ops:
  0.6 0.0 copy-start
  0.6 1.6 %copy-done = bf16[32,16,16,128]{3,2,1,0:T(8,128)(2,1)S(1)} copy-done((bf16[32,16,16,128]{3,2,1,0:T(8,128)(2,1)S(1)}, bf16[32,16,16,128]{3,2,1,0:T(8,128)(2,1)}, u32[]{:S(2)}) %copy-start) | copy-done | bytes 2097176
  2.2 0.0 copy-start.1
  2.2 0.7 copy-done.1
  2.9 0.0 copy-start.2
  2.9 0.7 copy-done.2
  3.7 70.3 %shard_map.85 = (f32[32,16,16,128]{3,2,1,0:T(8,128)S(1)}, bf16[32,16,16,128]{3,2,1,0:T(8,128)(2,1)S(1)}, f32[32,64]{1,0:T(8,128)S(1)}) custom-call(f32[32,16,16,128]{3,2,1,0:T(8,128)} %u_hbm.1, f32[32,16,16,128]{3,2,1,0:T(8,128)} %k_hbm.1, bf16[64,64]{1,0:T(8,128)(2,1)S(1)} %copy-done.1, bf16[64,16,16,128]{3,2,1,0:T(8,128)(2,1)} %psi_hbm.1, ...), custom_call_target="tpu_custom_call" | custom-call | tf_op jit(solution)/shard_map/pallas_call | solution.py:489
  74.0 2.7 %shard_map.86 = (f32[32,16,16,128]{3,2,1,0:T(8,128)}, bf16[32,16,16,128]{3,2,1,0:T(8,128)(2,1)}) custom-call(f32[32,16,16,128]{3,2,1,0:T(8,128)S(1)} %get-tuple-element.8.fin_ref, bf16[32,16,16,128]{3,2,1,0:T(8,128)(2,1)S(1)} %get-tuple-element.9.rng_ref), custom_call_target="tpu_custom_call" | custom-call | tf_op jit(solution)/shard_map/pallas_call | solution.py:503
  76.7 0.6 copy.10
Async XLA Ops:
  0.6 1.6 %copy-start = (bf16[32,16,16,128]{3,2,1,0:T(8,128)(2,1)S(1)}, bf16[32,16,16,128]{3,2,1,0:T(8,128)(2,1)}, u32[]{:S(2)}) copy-start(bf16[32,16,16,128]{3,2,1,0:T(8,128)(2,1)} %prev_hbm.1) | copy-start | bytes 6291460
  2.2 0.7 copy-start.1
  2.9 0.7 copy-start.2

commit v3 on v2

--- a/solution.py
+++ b/solution.py
@@ -16,21 +16,24 @@
 AHEAD = 16
 HELD = 4
 VMEM_MIB = 44
+PIECES = 4
+DETOUR = 1
+LAG = 3
 
 
 def kernel(
-    u_hbm, k_hbm, omega_ref, psi_hbm, prev_hbm, cprev_ref,
-    u_in, rout, cor_ref,
-    k_in, xs, xr, rly, ys, yr, snap, peer, psi, prev, acc, w_ref, red, part, gat1, part2, gat2,
+    u_hbm, k_hbm, omega_hbm, psi_hbm,
+    u_in, acc, cor_ref,
+    k_in, xs, xr, rly, rlp, ys, yr, snap, peer, psi, omega_ref, w_ref, red, part, gat1, part2, gat2,
     ua, ub, kk, cx, cy, cz, dd,
-    load_sem, aux_sem, xs_sem, xr_sem, ry_sem, rf_sem, ys_sem, yr_sem, ps_sem, pr_sem,
+    load_sem, aux_sem, xs_sem, xr_sem, ry_sem, rf_sem, ys_sem, yr_sem, ps_sem, pr_sem, ds_sem, dr_sem,
     a1s_sem, a1r_sem, a2s_sem, a2r_sem,
 ):
     S, X, Y, Z = u_in.shape
     NC = S // CHUNK
     XE = X + 2 * H
     R = psi.shape[0]
-    RD = prev.shape[0]
+    RD = acc.shape[1] // Y
     sx, sy, par = lax.axis_index("sx"), lax.axis_index("sy"), lax.axis_index("par")
     nsx, nsy = gat1.shape[0], gat2.shape[0]
     has = {("sx", 0): sx > 0, ("sx", 1): sx < nsx - 1, ("sy", 0): sy > 0, ("sy", 1): sy < nsy - 1}
@@ -104,15 +107,49 @@
             device_id={"par": 1 - par}, device_id_type=MESH,
         )
 
+    col = lax.rem(sx, XW)
+    outer = (col == 0) | (col == XW - 1)
+    pair = jnp.where(lax.rem(sx, 2) == 0, sx + 1, sx - 1)
+
+    def detours(c):
+        i = (c - NC // 2) // 2
+        return (c >= NC // 2) & (lax.rem(c, 2) == 0) & (i < DETOUR), i
+
+    def par_start(c):
+        takes, i = detours(c)
+        takes = takes & outer
+
+        @pl.when(takes)
+        def _():
+            pltpu.make_async_remote_copy(
+                snap.at[chunk(c)], rlp.at[i], ps_sem.at[c], dr_sem.at[i],
+                device_id={"sx": pair, "par": 1 - par}, device_id_type=MESH,
+            ).start()
+
+        @pl.when(jnp.logical_not(takes))
+        def _():
+            par_copy(c).start()
+
+    def pass_copy(c, i):
+        return remote(rlp.at[i], peer.at[chunk(c)], ds_sem.at[i], pr_sem.at[c], "sx", pair)
+
+    def par_pass(c):
+        due, i = detours(c)
+
+        @pl.when(due & jnp.logical_not(outer))
+        def _():
+            remote(rlp.at[i], rlp.at[i], ds_sem.at[i], dr_sem.at[i], "sx", pair).wait_recv()
+            pass_copy(c, i).start()
+
     @pl.loop(0, NC)
     def _(c):
         for cp in load(c):
             cp.start()
 
     psi_load = pltpu.make_async_copy(psi_hbm, psi, aux_sem.at[0])
-    prev_load = pltpu.make_async_copy(prev_hbm, prev, aux_sem.at[1])
+    omega_load = pltpu.make_async_copy(omega_hbm, omega_ref, aux_sem.at[1])
     psi_load.start()
-    prev_load.start()
+    omega_load.start()
 
     barrier = pltpu.get_barrier_semaphore()
     for d in range(1, nsx):
@@ -120,6 +157,7 @@
     for d in range(1, nsy):
         pl.semaphore_signal(barrier, inc=1, device_id={"sy": lax.rem(sy + d, nsy)}, device_id_type=MESH)
     pl.semaphore_signal(barrier, inc=1, device_id={"par": 1 - par}, device_id_type=MESH)
+    pl.semaphore_signal(barrier, inc=1, device_id={"sx": pair, "par": 1 - par}, device_id_type=MESH)
 
     for side in (0, 1):
         @pl.when(jnp.logical_not(has["sx", side]))
@@ -141,7 +179,7 @@
     cut = ((yrow == H - 1) & (sy == 0)) | ((yrow == H + Y - 1) & (sy == nsy - 1))
     ymask = jnp.where(cut, 0.0, 1.0).astype(F32)
 
-    pl.semaphore_wait(barrier, nsx + nsy - 1)
+    pl.semaphore_wait(barrier, nsx + nsy)
 
     def x_edges(c):
         for cp in load(c):
@@ -288,23 +326,6 @@
     relay(jnp.int32(2))
     y_edges(1)
 
-    i_r = lax.broadcasted_iota(jnp.int32, (RD * Y, R), 0) // Y
-    i_j = lax.broadcasted_iota(jnp.int32, (RD * Y, R), 1)
-    pick = jnp.where(i_j == i_r + par * RD, 1.0, 0.0).astype(BF16)
-    cols = lax.dot_general(pick, omega_ref[...], (((1,), (1,)), ((), ())), preferred_element_type=F32).astype(BF16)
-    total = omega_ref.shape[0]
-    WB = 256
-
-    @pl.loop(0, total * Y // WB)
-    def _(b):
-        e_s = lax.broadcasted_iota(jnp.int32, (total, WB), 0)
-        e_c = lax.broadcasted_iota(jnp.int32, (total, WB), 1) + b * WB
-        spread = jnp.where(e_s == lax.rem(e_c // Y + par * S, total), 1.0, 0.0).astype(BF16)
-        wide = jnp.dot(cols, spread, preferred_element_type=F32)
-        w_r = lax.rem(lax.broadcasted_iota(jnp.int32, (RD * Y, WB), 0), Y)
-        w_c = lax.rem(lax.broadcasted_iota(jnp.int32, (RD * Y, WB), 1), Y)
-        w_ref[:, pl.ds(pl.multiple_of(b * WB, WB), WB)] = jnp.where(w_r == w_c, wide, 0.0).astype(BF16)
-
     SB, RB = 16, 16
 
     def corange(sb):
@@ -355,7 +376,9 @@
 
         @pl.when(c < NC - HELD)
         def _():
-            par_copy(c).start()
+            par_start(c)
+
+        par_pass(c - LAG)
 
     corange(S // SB - 1)
 
@@ -379,9 +402,30 @@
 
     @pl.loop(NC - HELD, NC)
     def _(c):
-        par_copy(c).start()
-
-    prev_load.wait()
+        par_start(c)
+
+    @pl.loop(NC - LAG, NC)
+    def _(c):
+        par_pass(c)
+
+    omega_load.wait()
+    i_r = lax.broadcasted_iota(jnp.int32, (RD * Y, R), 0) // Y
+    i_j = lax.broadcasted_iota(jnp.int32, (RD * Y, R), 1)
+    pick = jnp.where(i_j == i_r + par * RD, 1.0, 0.0).astype(BF16)
+    cols = lax.dot_general(pick, omega_ref[...], (((1,), (1,)), ((), ())), preferred_element_type=F32).astype(BF16)
+    total = omega_ref.shape[0]
+    WB = 256
+
+    @pl.loop(0, total * Y // WB)
+    def _(b):
+        e_s = lax.broadcasted_iota(jnp.int32, (total, WB), 0)
+        e_c = lax.broadcasted_iota(jnp.int32, (total, WB), 1) + b * WB
+        spread = jnp.where(e_s == lax.rem(e_c // Y + par * S, total), 1.0, 0.0).astype(BF16)
+        wide = jnp.dot(cols, spread, preferred_element_type=F32)
+        w_r = lax.rem(lax.broadcasted_iota(jnp.int32, (RD * Y, WB), 0), Y)
+        w_c = lax.rem(lax.broadcasted_iota(jnp.int32, (RD * Y, WB), 1), Y)
+        w_ref[:, pl.ds(pl.multiple_of(b * WB, WB), WB)] = jnp.where(w_r == w_c, wide, 0.0).astype(BF16)
+
 
     def range_part(x0, weights, source, lo, n):
         right = jnp.concatenate([source[lo:lo + n, x0 + d].reshape(n * Y, Z) for d in range(2)], axis=1)
@@ -390,7 +434,7 @@
     for x0 in range(0, X, 2):
         t = range_part(x0, w_ref[:, 0:S * Y], snap, 0, S)
         for d in range(2):
-            acc[x0 + d] = prev[:, x0 + d].reshape(RD * Y, Z).astype(F32) + t[:, d * Z:(d + 1) * Z]
+            acc[x0 + d] = t[:, d * Z:(d + 1) * Z]
 
     gat1[pl.ds(sx, 1)] = part[...][None]
     for d in range(1, nsx):
@@ -419,7 +463,7 @@
     for i in range(1, nsy):
         tot += gat2[i]
     for q in range(S // SB):
-        cor_ref[q * SB:(q + 1) * SB] = cprev_ref[q * SB:(q + 1) * SB] + tot[:, q * R:(q + 1) * R]
+        cor_ref[q * SB:(q + 1) * SB] = tot[:, q * R:(q + 1) * R]
 
     for c in range(NC // 2, NC):
         par_copy(c).wait_recv()
@@ -427,8 +471,7 @@
     for x0 in range(0, X, 2):
         t = range_part(x0, w_ref[:, (S + HALF) * Y:2 * S * Y], peer, HALF, HALF)
         for d in range(2):
-            v = acc[x0 + d] + t[:, d * Z:(d + 1) * Z]
-            rout[:, x0 + d] = v.astype(BF16).reshape(RD, Y, Z)
+            acc[x0 + d] = acc[x0 + d] + t[:, d * Z:(d + 1) * Z]
 
     @pl.loop(0, NC)
     def _(c):
@@ -438,18 +481,36 @@
                 def _():
                     halo(axis, side, c).wait_send()
         relay_done(c)
+        due, i = detours(c)
+
+        @pl.when(due & jnp.logical_not(outer))
+        def _():
+            pass_copy(c, i).wait_send()
+
         par_copy(c).wait_send()
 
 
-def store(fin_ref, rng_ref, fin_hbm, rng_hbm, sem):
-    parts = 4
-    copies = []
-    for i, (src, dst) in enumerate(((fin_ref, fin_hbm), (rng_ref, rng_hbm))):
-        n = src.shape[0] // parts
-        copies += [pltpu.make_async_copy(src.at[pl.ds(p * n, n)], dst.at[pl.ds(p * n, n)], sem.at[i, p]) for p in range(parts)]
-    for cp in copies:
+def store(fin_ref, acc_ref, cor_ref, prev_hbm, cprev_ref, fin_hbm, rng_hbm, cor_out, prev, rng, sem):
+    RD, X, Y, Z = prev.shape
+    N = PIECES
+    n, m = RD // N, fin_ref.shape[0] // N
+    loads = [pltpu.make_async_copy(prev_hbm.at[pl.ds(p * n, n)], prev.at[pl.ds(p * n, n)], sem.at[0, p]) for p in range(N)]
+    fins = [pltpu.make_async_copy(fin_ref.at[pl.ds(p * m, m)], fin_hbm.at[pl.ds(p * m, m)], sem.at[1, p]) for p in range(N)]
+    outs = [pltpu.make_async_copy(rng.at[pl.ds(p * n, n)], rng_hbm.at[pl.ds(p * n, n)], sem.at[2, p]) for p in range(N)]
+    for cp in loads + fins:
         cp.start()
-    for cp in copies:
+    cor_out[...] = cprev_ref[...] + cor_ref[...]
+    for p in range(N):
+        loads[p].wait()
+
+        def add(x, _, p=p):
+            new = acc_ref[x, p * n * Y:(p + 1) * n * Y].reshape(n, Y, Z)
+            rng[p * n:(p + 1) * n, x] = (prev[p * n:(p + 1) * n, x].astype(F32) + new).astype(BF16)
+            return 0
+
+        lax.fori_loop(0, X, add, 0, unroll=True)
+        outs[p].start()
+    for cp in fins + outs:
         cp.wait()
 
 
@@ -465,13 +526,13 @@
         pltpu.VMEM((2, S, 2 * H, Y, Z), BF16),
         pltpu.VMEM((2, S, 2 * H, Y, Z), BF16),
         pltpu.VMEM((NC // 2, CHUNK, 2 * H, Y, Z), BF16),
+        pltpu.VMEM((DETOUR, CHUNK, X, Y, Z), BF16),
         pltpu.VMEM((2, S, E[0] // 2, 16, Z), BF16),
         pltpu.VMEM((2, S, E[0] // 2, 16, Z), BF16),
         pltpu.VMEM((S, X, Y, Z), BF16),
         pltpu.VMEM((S, X, Y, Z), BF16),
         pltpu.VMEM((R, X, Y, Z), BF16),
-        pltpu.VMEM((RD, X, Y, Z), BF16),
-        pltpu.VMEM((X, RD * Y, Z), F32),
+        pltpu.VMEM(omega.shape, BF16),
         pltpu.VMEM((RD * Y, 2 * S * Y), BF16),
         pltpu.VMEM((S // 16, R, 16 * Y), F32),
         pltpu.VMEM((R * S // Z, Z), F32),
@@ -480,7 +541,7 @@
         pltpu.VMEM((nsy, R * S // Z, Z), F32),
     ] + [pltpu.VMEM(E, F32)] * 7 + [
         dma((2, NC)), dma((2,)), dma((2, NC)), dma((2, NC)), dma((NC // 2,)), dma((NC // 2,)),
-        dma((2, NC)), dma((2, NC)), dma((NC,)), dma((NC,)),
+        dma((2, NC)), dma((2, NC)), dma((NC,)), dma((NC,)), dma((DETOUR,)), dma((DETOUR,)),
         dma((nsx,)), dma((nsx,)), dma((nsy,)), dma((nsy,)),
     ]
     any_ = pl.BlockSpec(memory_space=pl.ANY)
@@ -490,27 +551,28 @@
         kernel,
         out_shape=(
             jax.ShapeDtypeStruct(initial_state.shape, F32),
-            jax.ShapeDtypeStruct(range_prev.shape, BF16),
+            jax.ShapeDtypeStruct((X, RD * Y, Z), F32),
             jax.ShapeDtypeStruct(corange_prev.shape[::-1], F32),
         ),
-        in_specs=[hbm, hbm, vmem, hbm, hbm, vmem],
+        in_specs=[hbm, hbm, hbm, hbm],
         out_specs=(vmem, vmem, vmem),
         scratch_shapes=scratch,
         compiler_params=pltpu.CompilerParams(
             collective_id=0, has_side_effects=True, vmem_limit_bytes=VMEM_MIB * 2**20
         ),
-    )(initial_state, conductivity, omega, psi, range_prev, corange_prev.T)
-    final, sketch = pl.pallas_call(
+    )(initial_state, conductivity, omega, psi)
+    final, sketch, corange = pl.pallas_call(
         store,
         out_shape=(
             jax.ShapeDtypeStruct(initial_state.shape, F32),
             jax.ShapeDtypeStruct(range_prev.shape, BF16),
+            jax.ShapeDtypeStruct(corange_prev.shape[::-1], F32),
         ),
-        in_specs=[vmem, vmem],
-        out_specs=(any_, any_),
-        scratch_shapes=[dma((2, 4))],
-        compiler_params=pltpu.CompilerParams(vmem_limit_bytes=8 * 2**20),
-    )(final, sketch)
+        in_specs=[vmem, vmem, vmem, any_, vmem],
+        out_specs=(any_, any_, vmem),
+        scratch_shapes=[pltpu.VMEM(range_prev.shape, BF16), pltpu.VMEM(range_prev.shape, BF16), dma((3, PIECES))],
+        compiler_params=pltpu.CompilerParams(vmem_limit_bytes=16 * 2**20),
+    )(final, sketch, corange, range_prev, corange_prev.T)
     return final, sketch, corange.T
 
 

time: 77.6 us -> 73.4 us (0.946)
  local copies, waits for them, and re-layouts: 3.63 us -> 0.72 us
  Pallas kernels: 73 us -> 71.1 us
    unnamed x7 -> x6, local copies, waits for them, and re-layouts: 3.63 us -> 0.72 us
    pallas_call x1, Pallas kernels: 70.3 us -> 67.6 us  [per_device(): pl.pallas_call(kernel, out_shape=(jax.ShapeDtypeStruct(initial_state.shap...]
    pallas_call x1, Pallas kernels: 2.72 us -> 3.5 us  [per_device(): pl.pallas_call(store, out_shape=(jax.ShapeDtypeStruct(initial_state.shape...]
where the time goes in v3:
time: 73.4 us; the launch traced here: 72.5 us
  Pallas kernels  71.1 us (97%)
    pallas_call x1, Pallas kernels, per_device(): pl.pallas_call(kernel, out_shape=(jax.ShapeDtypeStruct(initial_state.shap...  67.6 us
    pallas_call x1, Pallas kernels, per_device(): pl.pallas_call(store, out_shape=(jax.ShapeDtypeStruct(initial_state.shape...  3.5 us

profile of v3, /device:TPU:1, one launch (start us, length us, event | category | flops | bytes accessed | tf_op | source)
XLA Modules:
  0.0 72.5 jit_solution(7340321516163973869)
XLA Ops:
  0.6 0.0 copy-start.1
  0.6 0.7 copy-done.1
  1.4 0.0 copy-start
  1.4 0.0 copy-start.2
  1.4 67.6 %shard_map.85 = (f32[32,16,16,128]{3,2,1,0:T(8,128)S(1)}, f32[16,512,128]{2,1,0:T(8,128)S(1)}, f32[32,64]{1,0:T(8,128)S(1)}) custom-call(f32[32,16,16,128]{3,2,1,0:T(8,128)} %u_hbm.1, f32[32,16,16,128]{3,2,1,0:T(8,128)} %k_hbm.1, bf16[64,64]{1,0:T(8,128)(2,1)S(1)} %copy-done.1, bf16[64,16,16,128]{3,2,1,0:T(8,128)(2,1)} %psi_hbm.1), custom_call_target="tpu_custom_call" | custom-call | tf_op jit(solution)/shard_map/pallas_call | solution.py:550
  69.0 0.0 copy-done
  69.0 0.0 copy-done.2
  69.0 3.5 %shard_map.86 = (f32[32,16,16,128]{3,2,1,0:T(8,128)}, bf16[32,16,16,128]{3,2,1,0:T(8,128)(2,1)}, f32[32,64]{1,0:T(8,128)}) custom-call(f32[32,16,16,128]{3,2,1,0:T(8,128)S(1)} %get-tuple-element.9.fin_ref, f32[16,512,128]{2,1,0:T(8,128)S(1)} %get-tuple-element.10.acc_ref, f32[32,64]{1,0:T(8,128)S(1)} %get-tuple-element.11.cor_ref, ...), custom_call_target="tpu_custom_call" | custom-call | tf_op jit(solution)/shard_map/pallas_call | solution.py:564
Async XLA Ops:
  0.6 0.7 copy-start.1
  1.4 67.7 %copy-start = (bf16[32,16,16,128]{3,2,1,0:T(8,128)(2,1)S(1)}, bf16[32,16,16,128]{3,2,1,0:T(8,128)(2,1)}, u32[]{:S(2)}) copy-start(bf16[32,16,16,128]{3,2,1,0:T(8,128)(2,1)} %prev_hbm.1) | copy-start | bytes 6291460
  1.4 67.7 %copy-start.2 = (f32[64,32]{0,1:T(8,128)S(1)}, f32[64,32]{0,1:T(8,128)}, u32[]{:S(2)}) copy-start(f32[64,32]{0,1:T(8,128)} %param.11) | copy-start | bytes 24580

commit v4 on v3

--- a/solution.py
+++ b/solution.py
@@ -560,7 +560,7 @@
         compiler_params=pltpu.CompilerParams(
             collective_id=0, has_side_effects=True, vmem_limit_bytes=VMEM_MIB * 2**20
         ),
-    )(initial_state, conductivity, omega, psi)
+    )(initial_state, conductivity, pltpu.with_memory_space_constraint(omega, pltpu.HBM), psi)
     final, sketch, corange = pl.pallas_call(
         store,
         out_shape=(

time: 73.4 us -> 72.7 us (level)
  no operation moved by 1% of the time
where the time goes in v4:
time: 72.7 us; the launch traced here: 71.9 us
  Pallas kernels  71.2 us (98%)
    pallas_call x1, Pallas kernels, per_device(): pl.pallas_call(kernel, out_shape=(jax.ShapeDtypeStruct(initial_state.shap...  67.7 us
    pallas_call x1, Pallas kernels, per_device(): pl.pallas_call(store, out_shape=(jax.ShapeDtypeStruct(initial_state.shape...  3.5 us

profile of v4, /device:TPU:1, one launch (start us, length us, event | category | flops | bytes accessed | tf_op | source)
XLA Modules:
  0.0 71.9 jit_solution(7764005091994815773)
XLA Ops:
  0.6 0.0 copy-start
  0.6 0.0 copy-start.1
  0.7 67.7 %shard_map.85 = (f32[32,16,16,128]{3,2,1,0:T(8,128)S(1)}, f32[16,512,128]{2,1,0:T(8,128)S(1)}, f32[32,64]{1,0:T(8,128)S(1)}) custom-call(f32[32,16,16,128]{3,2,1,0:T(8,128)} %u_hbm.1, f32[32,16,16,128]{3,2,1,0:T(8,128)} %k_hbm.1, bf16[64,64]{1,0:T(8,128)(2,1)} %omega_hbm.1, bf16[64,16,16,128]{3,2,1,0:T(8,128)(2,1)} %psi_hbm.1), custom_call_target="tpu_custom_call" | custom-call | tf_op jit(solution)/shard_map/pallas_call | solution.py:550
  68.4 0.0 copy-done
  68.4 0.0 copy-done.1
  68.4 3.5 %shard_map.86 = (f32[32,16,16,128]{3,2,1,0:T(8,128)}, bf16[32,16,16,128]{3,2,1,0:T(8,128)(2,1)}, f32[32,64]{1,0:T(8,128)}) custom-call(f32[32,16,16,128]{3,2,1,0:T(8,128)S(1)} %get-tuple-element.9.fin_ref, f32[16,512,128]{2,1,0:T(8,128)S(1)} %get-tuple-element.10.acc_ref, f32[32,64]{1,0:T(8,128)S(1)} %get-tuple-element.11.cor_ref, ...), custom_call_target="tpu_custom_call" | custom-call | tf_op jit(solution)/shard_map/pallas_call | solution.py:564
Async XLA Ops:
  0.6 67.8 %copy-start = (bf16[32,16,16,128]{3,2,1,0:T(8,128)(2,1)S(1)}, bf16[32,16,16,128]{3,2,1,0:T(8,128)(2,1)}, u32[]{:S(2)}) copy-start(bf16[32,16,16,128]{3,2,1,0:T(8,128)(2,1)} %prev_hbm.1) | copy-start | bytes 6291460
  0.6 67.8 %copy-start.1 = (f32[64,32]{0,1:T(8,128)S(1)}, f32[64,32]{0,1:T(8,128)}, u32[]{:S(2)}) copy-start(f32[64,32]{0,1:T(8,128)} %param.11) | copy-start | bytes 24580

commit v5 on v4

--- a/solution.py
+++ b/solution.py
@@ -68,18 +68,18 @@
                       axis, beside(axis, side))
 
     def detour(side, c):
-        q = lax.rem(c, 2) * (XW - 1)
+        q = jnp.where(c >= NC // 2, XW - 1, 0)
         at_seam = (sx == XW - 1) if side == 1 else (sx == XW)
         via = XW + q if side == 1 else XW - 1 - q
-        return at_seam & (q != 0), via, c // 2
+        return at_seam & (q != 0), via, lax.rem(c, NC // 2)
 
     def to_relay(side, c):
         _, via, m = detour(side, c)
         return remote(xs.at[side, chunk(c)], rly.at[m], xs_sem.at[side, c], ry_sem.at[m], "sx", via)
 
     def relay(c):
-        q = lax.rem(c, 2) * (XW - 1)
-        m = c // 2
+        q = jnp.where(c >= NC // 2, XW - 1, 0)
+        m = lax.rem(c, NC // 2)
         for side in (0, 1):
             mine = ((sx == XW + q) if side == 1 else (sx == XW - 1 - q)) & (q != 0)
 
@@ -91,8 +91,8 @@
                 cp.start()
 
     def relay_done(c):
-        q = lax.rem(c, 2) * (XW - 1)
-        m = c // 2
+        q = jnp.where(c >= NC // 2, XW - 1, 0)
+        m = lax.rem(c, NC // 2)
         for side in (0, 1):
             mine = ((sx == XW + q) if side == 1 else (sx == XW - 1 - q)) & (q != 0)
 
@@ -112,8 +112,8 @@
     pair = jnp.where(lax.rem(sx, 2) == 0, sx + 1, sx - 1)
 
     def detours(c):
-        i = (c - NC // 2) // 2
-        return (c >= NC // 2) & (lax.rem(c, 2) == 0) & (i < DETOUR), i
+        i = (c - (NC - 6)) // 2
+        return (c >= NC - 6) & (lax.rem(c, 2) == 0) & (i < DETOUR), i
 
     def par_start(c):
         takes, i = detours(c)
@@ -490,19 +490,16 @@
         par_copy(c).wait_send()
 
 
-def store(fin_ref, acc_ref, cor_ref, prev_hbm, cprev_ref, fin_hbm, rng_hbm, cor_out, prev, rng, sem):
+def store(fin_ref, acc_ref, cor_ref, prev, cprev_ref, fin_hbm, rng_hbm, cor_out, rng, sem):
     RD, X, Y, Z = prev.shape
     N = PIECES
     n, m = RD // N, fin_ref.shape[0] // N
-    loads = [pltpu.make_async_copy(prev_hbm.at[pl.ds(p * n, n)], prev.at[pl.ds(p * n, n)], sem.at[0, p]) for p in range(N)]
-    fins = [pltpu.make_async_copy(fin_ref.at[pl.ds(p * m, m)], fin_hbm.at[pl.ds(p * m, m)], sem.at[1, p]) for p in range(N)]
-    outs = [pltpu.make_async_copy(rng.at[pl.ds(p * n, n)], rng_hbm.at[pl.ds(p * n, n)], sem.at[2, p]) for p in range(N)]
-    for cp in loads + fins:
+    fins = [pltpu.make_async_copy(fin_ref.at[pl.ds(p * m, m)], fin_hbm.at[pl.ds(p * m, m)], sem.at[0, p]) for p in range(N)]
+    outs = [pltpu.make_async_copy(rng.at[pl.ds(p * n, n)], rng_hbm.at[pl.ds(p * n, n)], sem.at[1, p]) for p in range(N)]
+    for cp in fins:
         cp.start()
     cor_out[...] = cprev_ref[...] + cor_ref[...]
     for p in range(N):
-        loads[p].wait()
-
         def add(x, _, p=p):
             new = acc_ref[x, p * n * Y:(p + 1) * n * Y].reshape(n, Y, Z)
             rng[p * n:(p + 1) * n, x] = (prev[p * n:(p + 1) * n, x].astype(F32) + new).astype(BF16)
@@ -568,9 +565,9 @@
             jax.ShapeDtypeStruct(range_prev.shape, BF16),
             jax.ShapeDtypeStruct(corange_prev.shape[::-1], F32),
         ),
-        in_specs=[vmem, vmem, vmem, any_, vmem],
+        in_specs=[vmem, vmem, vmem, vmem, vmem],
         out_specs=(any_, any_, vmem),
-        scratch_shapes=[pltpu.VMEM(range_prev.shape, BF16), pltpu.VMEM(range_prev.shape, BF16), dma((3, PIECES))],
+        scratch_shapes=[pltpu.VMEM(range_prev.shape, BF16), dma((2, PIECES))],
         compiler_params=pltpu.CompilerParams(vmem_limit_bytes=16 * 2**20),
     )(final, sketch, corange, range_prev, corange_prev.T)
     return final, sketch, corange.T

time: 72.7 us -> 72.5 us (level)
  no operation moved by 1% of the time
where the time goes in v5:
time: 72.5 us; the launch traced here: 71.7 us
  Pallas kernels  71 us (98%)
    pallas_call x1, Pallas kernels, per_device(): pl.pallas_call(kernel, out_shape=(jax.ShapeDtypeStruct(initial_state.shap...  67.7 us
    pallas_call x1, Pallas kernels, per_device(): pl.pallas_call(store, out_shape=(jax.ShapeDtypeStruct(initial_state.shape...  3.32 us

profile of v5, /device:TPU:1, one launch (start us, length us, event | category | flops | bytes accessed | tf_op | source)
XLA Modules:
  0.0 71.7 jit_solution(4444337007371909440)
XLA Ops:
  0.6 0.0 copy-start
  0.6 0.0 copy-start.1
  0.7 67.7 %shard_map.85 = (f32[32,16,16,128]{3,2,1,0:T(8,128)S(1)}, f32[16,512,128]{2,1,0:T(8,128)S(1)}, f32[32,64]{1,0:T(8,128)S(1)}) custom-call(f32[32,16,16,128]{3,2,1,0:T(8,128)} %u_hbm.1, f32[32,16,16,128]{3,2,1,0:T(8,128)} %k_hbm.1, bf16[64,64]{1,0:T(8,128)(2,1)} %omega_hbm.1, bf16[64,16,16,128]{3,2,1,0:T(8,128)(2,1)} %psi_hbm.1), custom_call_target="tpu_custom_call" | custom-call | tf_op jit(solution)/shard_map/pallas_call | solution.py:547
  68.4 0.0 copy-done
  68.4 0.0 copy-done.1
  68.4 3.3 %shard_map.86 = (f32[32,16,16,128]{3,2,1,0:T(8,128)}, bf16[32,16,16,128]{3,2,1,0:T(8,128)(2,1)}, f32[32,64]{1,0:T(8,128)}) custom-call(f32[32,16,16,128]{3,2,1,0:T(8,128)S(1)} %get-tuple-element.9.fin_ref, f32[16,512,128]{2,1,0:T(8,128)S(1)} %get-tuple-element.10.acc_ref, f32[32,64]{1,0:T(8,128)S(1)} %get-tuple-element.11.cor_ref, ...), custom_call_target="tpu_custom_call" | custom-call | tf_op jit(solution)/shard_map/pallas_call | solution.py:561
Async XLA Ops:
  0.6 67.7 %copy-start = (bf16[32,16,16,128]{3,2,1,0:T(8,128)(2,1)S(1)}, bf16[32,16,16,128]{3,2,1,0:T(8,128)(2,1)}, u32[]{:S(2)}) copy-start(bf16[32,16,16,128]{3,2,1,0:T(8,128)(2,1)} %prev.1) | copy-start | bytes 6291460
  0.6 67.7 %copy-start.1 = (f32[64,32]{0,1:T(8,128)S(1)}, f32[64,32]{0,1:T(8,128)}, u32[]{:S(2)}) copy-start(f32[64,32]{0,1:T(8,128)} %param.11) | copy-start | bytes 24580

commit v6 on v5

--- a/solution.py
+++ b/solution.py
@@ -16,7 +16,7 @@
 AHEAD = 16
 HELD = 4
 VMEM_MIB = 44
-PIECES = 4
+PIECES = 2
 DETOUR = 1
 LAG = 3
 

time: 72.5 us -> 72.5 us (level)
  no operation moved by 1% of the time
where the time goes in v6:
time: 72.5 us; the launch traced here: 71.7 us
  Pallas kernels  71 us (98%)
    pallas_call x1, Pallas kernels, per_device(): pl.pallas_call(kernel, out_shape=(jax.ShapeDtypeStruct(initial_state.shap...  67.7 us
    pallas_call x1, Pallas kernels, per_device(): pl.pallas_call(store, out_shape=(jax.ShapeDtypeStruct(initial_state.shape...  3.31 us

profile of v6, /device:TPU:1, one launch (start us, length us, event | category | flops | bytes accessed | tf_op | source)
XLA Modules:
  0.0 71.7 jit_solution(11566881249935550934)
XLA Ops:
  0.6 0.0 copy-start
  0.6 0.0 copy-start.1
  0.7 67.7 %shard_map.85 = (f32[32,16,16,128]{3,2,1,0:T(8,128)S(1)}, f32[16,512,128]{2,1,0:T(8,128)S(1)}, f32[32,64]{1,0:T(8,128)S(1)}) custom-call(f32[32,16,16,128]{3,2,1,0:T(8,128)} %u_hbm.1, f32[32,16,16,128]{3,2,1,0:T(8,128)} %k_hbm.1, bf16[64,64]{1,0:T(8,128)(2,1)} %omega_hbm.1, bf16[64,16,16,128]{3,2,1,0:T(8,128)(2,1)} %psi_hbm.1), custom_call_target="tpu_custom_call" | custom-call | tf_op jit(solution)/shard_map/pallas_call | solution.py:547
  68.4 0.0 copy-done
  68.4 0.0 copy-done.1
  68.4 3.3 %shard_map.86 = (f32[32,16,16,128]{3,2,1,0:T(8,128)}, bf16[32,16,16,128]{3,2,1,0:T(8,128)(2,1)}, f32[32,64]{1,0:T(8,128)}) custom-call(f32[32,16,16,128]{3,2,1,0:T(8,128)S(1)} %get-tuple-element.9.fin_ref, f32[16,512,128]{2,1,0:T(8,128)S(1)} %get-tuple-element.10.acc_ref, f32[32,64]{1,0:T(8,128)S(1)} %get-tuple-element.11.cor_ref, ...), custom_call_target="tpu_custom_call" | custom-call | tf_op jit(solution)/shard_map/pallas_call | solution.py:561
Async XLA Ops:
  0.6 67.7 %copy-start = (bf16[32,16,16,128]{3,2,1,0:T(8,128)(2,1)S(1)}, bf16[32,16,16,128]{3,2,1,0:T(8,128)(2,1)}, u32[]{:S(2)}) copy-start(bf16[32,16,16,128]{3,2,1,0:T(8,128)(2,1)} %prev.1) | copy-start | bytes 6291460
  0.6 67.7 %copy-start.1 = (f32[64,32]{0,1:T(8,128)S(1)}, f32[64,32]{0,1:T(8,128)}, u32[]{:S(2)}) copy-start(f32[64,32]{0,1:T(8,128)} %param.11) | copy-start | bytes 24580
